TPU v7x, 256 devices: a whole 4x4x8 slice. The times are simulated.
256 devices in a mesh: segment: 2 (over y_lo), tm: 8 (over z), rows: 16 (over y_hi, x, core).
Axes of the slice: x: 4, y: 4 (y_hi: 2, y_lo: 2; y = y_hi * 2 + y_lo), z: 8, core: 2. Of those that a mesh axis runs over, the one named last changes fastest.
Arguments:
- input_clip: bfloat16 [16, 32, 128, 128], P('tm', 'rows'), may hold values from -6 to 6
- cotangent: bfloat16 [16, 32, 128, 128], P('tm', 'rows'), may hold values from -0.046875 to 0.046875
- kernel_in: bfloat16 [2, 3456, 256], P('segment'), may hold values from -0.109375 to 0.109375
- kernel_out: bfloat16 [2, 6912, 128], P('segment'), may hold values from -0.078125 to 0.078125
Outputs:
- sections: bfloat16 [2, 16, 32, 128, 128], P('segment', 'tm', 'rows')
- grad_in: float32 [2, 884736], P('segment', ('tm', 'rows'))
- grad_out: float32 [2, 884736], P('segment', ('tm', 'rows'))
All inputs are finite; a program needn't handle non-finite values.
Results may differ from a plain program's by a relative error of at most 0.007.
Values may be sent and summed in bfloat16 or wider, within the bound.
A program may use at most 128 MiB of HBM per device.

v0:
```python
from functools import partial

import jax
import jax.numpy as jnp
from jax import lax
from jax.experimental import pallas as pl
from jax.experimental.pallas import tpu as pltpu
from jax.sharding import PartitionSpec as P

MESH_ID = pl.DeviceIdType.MESH
CORES, XS, YS, ZS = 2, 4, 2, 8
CHUNK = 112


def reduce_scatter_kernel(
    b_ref, in_ref, out_ref, got_core, half, got_x, mine, quarter, got_z, last, got_y,
    send_core, recv_core, send_x, recv_x, send_z, recv_z, send_y, recv_y,
):
    row = lax.axis_index("rows")
    tm = lax.axis_index("tm")
    core = lax.rem(row, 2)
    at_x = lax.rem(row // 2, 4)
    at_y = row // 8

    def row_of(y, x, c):
        return y * 8 + x * 2 + c

    def x_at(offset):
        return lax.rem(at_x + offset, XS)

    def z_at(offset):
        return lax.rem(tm + offset, ZS)

    sibling = {"rows": row_of(at_y, at_x, 1 - core)}
    across_y = {"rows": row_of(1 - at_y, at_x, core)}
    barrier = pltpu.get_barrier_semaphore()
    partners = [sibling, across_y]
    partners += [{"rows": row_of(at_y, x_at(o), core)} for o in range(1, XS)]
    partners += [{"tm": z_at(p)} for p in range(1, ZS)]
    for partner in partners:
        pl.semaphore_signal(barrier, inc=1, device_id=partner, device_id_type=MESH_ID)
    pl.semaphore_wait(barrier, len(partners))

    order = (2, 1, 3, 0)
    core_copies = {}
    for o in order:
        copy = pltpu.make_async_remote_copy(
            src_ref=b_ref.at[:, :, x_at(o), 1 - core],
            dst_ref=got_core.at[o],
            send_sem=send_core.at[o],
            recv_sem=recv_core.at[o],
            device_id=sibling,
            device_id_type=MESH_ID,
        )
        copy.start()
        core_copies[o] = copy
    x_copies = []
    for o in order:
        core_copies[o].wait_recv()
        x = x_at(o)

        def add_core(z, carry, o=o, x=x):
            total = b_ref[z, :, x, core].astype(jnp.float32) + got_core[o, z].astype(jnp.float32)
            if o == 0:
                mine[z] = total
            else:
                half[o, z] = total.astype(jnp.bfloat16)
            return carry

        lax.fori_loop(0, ZS, add_core, 0)
        if o:
            copy = pltpu.make_async_remote_copy(
                src_ref=half.at[o],
                dst_ref=got_x.at[o],
                send_sem=send_x.at[o],
                recv_sem=recv_x.at[o],
                device_id={"rows": row_of(at_y, x, core)},
                device_id_type=MESH_ID,
            )
            copy.start()
            x_copies.append(copy)
    for copy in x_copies:
        copy.wait_recv()
    z_copies = []
    for p in (4, 3, 5, 2, 6, 1, 7, 0):
        z = z_at(p)
        total = mine[z]
        for o in range(1, XS):
            total = total + got_x[o, z].astype(jnp.float32)
        if p == 0:
            mine[z] = total
        else:
            quarter[p] = total.astype(jnp.bfloat16)
            copy = pltpu.make_async_remote_copy(
                src_ref=quarter.at[p],
                dst_ref=got_z.at[p],
                send_sem=send_z.at[p],
                recv_sem=recv_z.at[p],
                device_id={"tm": z},
                device_id_type=MESH_ID,
            )
            copy.start()
            z_copies.append(copy)
    for copy in z_copies:
        copy.wait_recv()
    for side in range(YS):
        total = mine[tm, side]
        for p in range(1, ZS):
            total = total + got_z[p, side].astype(jnp.float32)
        mine[tm, side] = total
    last[...] = mine[tm, 1 - at_y].astype(jnp.bfloat16)
    copy = pltpu.make_async_remote_copy(
        src_ref=last,
        dst_ref=got_y,
        send_sem=send_y,
        recv_sem=recv_y,
        device_id=across_y,
        device_id_type=MESH_ID,
    )
    copy.start()
    copy.wait_recv()
    total = mine[tm, at_y] + got_y[...].astype(jnp.float32)
    in_ref[:, 0:128] = total[0:27]
    in_ref[:, 128:256] = total[27:54]
    out_ref[...] = total[54:108]
    for copy in [core_copies[o] for o in order] + x_copies + z_copies + [copy]:
        copy.wait_send()


def reduce_scatter(blocks):
    whole = pl.BlockSpec(memory_space=pltpu.VMEM)
    tile = (CHUNK, 128)
    dma = pltpu.SemaphoreType.DMA
    return pl.pallas_call(
        reduce_scatter_kernel,
        out_shape=(
            jax.ShapeDtypeStruct((27, 256), jnp.float32),
            jax.ShapeDtypeStruct((54, 128), jnp.float32),
        ),
        in_specs=[whole],
        out_specs=(whole, whole),
        scratch_shapes=[
            pltpu.VMEM((XS, ZS, YS) + tile, jnp.bfloat16),
            pltpu.VMEM((XS, ZS, YS) + tile, jnp.bfloat16),
            pltpu.VMEM((XS, ZS, YS) + tile, jnp.bfloat16),
            pltpu.VMEM((ZS, YS) + tile, jnp.float32),
            pltpu.VMEM((ZS, YS) + tile, jnp.bfloat16),
            pltpu.VMEM((ZS, YS) + tile, jnp.bfloat16),
            pltpu.VMEM(tile, jnp.bfloat16),
            pltpu.VMEM(tile, jnp.bfloat16),
            dma((XS,)), dma((XS,)), dma((XS,)), dma((XS,)), dma((ZS,)), dma((ZS,)), dma, dma,
        ],
        compiler_params=pltpu.CompilerParams(
            collective_id=0, has_side_effects=True, vmem_limit_bytes=40 << 20
        ),
    )(blocks)


def shifted(line, by):
    rows = lax.broadcasted_iota(jnp.int32, line.shape, 0)
    if by == 1:
        return jnp.where(rows == 0, 0.0, pltpu.roll(line, 1, 0))
    return jnp.where(rows == 127, 0.0, pltpu.roll(line, 127, 0))


def joined(low, mid, high, reverse):
    if reverse:
        return shifted(low, -1) + mid + shifted(high, 1)
    return shifted(low, 1) + mid + shifted(high, -1)


class Link:
    def __init__(self, src, dst, sems, index, device, sends, receives):
        self.parts = (src, dst, sems[0].at[index], sems[1].at[index], device)
        self.sends = sends
        self.receives = receives

    def copy(self):
        src, dst, send_sem, recv_sem, device = self.parts
        return pltpu.make_async_remote_copy(
            src_ref=src, dst_ref=dst, send_sem=send_sem, recv_sem=recv_sem,
            device_id=device, device_id_type=MESH_ID,
        )

    def start(self):
        @pl.when(self.sends)
        def _():
            self.copy().start()

    def wait_recv(self):
        @pl.when(self.receives)
        def _():
            self.copy().wait_recv()

    def wait_send(self):
        @pl.when(self.sends)
        def _():
            self.copy().wait_send()


def front_kernel(
    tms, rows_count, x_ref, g_ref, kin_ref, kout_ref, sect_ref, b_ref,
    back_ref, xp, gp, icx, icg, acc, hid, dgrad, act, gate, window, inner,
    sent_f, got_f, sum_f, got_zf, sent_b, got_b, sum_b, got_zb,
    wide_e, wide_a, fin, fout,
    s_xp, r_xp, s_gp, r_gp, s_sf, r_sf, s_sb, r_sb, s_seg, r_seg,
):
    seg = lax.axis_index("segment")
    tm = lax.axis_index("tm")
    row = lax.axis_index("rows")
    encodes = seg == 0
    decodes = seg == 1
    up, down = row + 1 < rows_count, row > 0
    later, earlier = tm + 1 < tms, tm > 0
    row_up = {"rows": lax.rem(row + 1, rows_count)}
    row_down = {"rows": lax.rem(row + rows_count - 1, rows_count)}
    tm_later = {"tm": lax.rem(tm + 1, tms)}
    tm_earlier = {"tm": lax.rem(tm + tms - 1, tms)}
    other = {"segment": 1 - seg}
    both = jnp.logical_and

    xp[...] = jnp.zeros_like(xp)
    gp[...] = jnp.zeros_like(gp)
    got_f[...] = jnp.zeros_like(got_f)
    got_zf[...] = jnp.zeros_like(got_zf)
    got_b[...] = jnp.zeros_like(got_b)
    got_zb[...] = jnp.zeros_like(got_zb)

    @pl.when(encodes)
    def _():
        xp[2:4, 1:3] = x_ref[...]

    @pl.when(decodes)
    def _():
        gp[0:2, 1:3] = g_ref[...]

    barrier = pltpu.get_barrier_semaphore()
    for partner in (row_up, row_down, tm_later, tm_earlier, other):
        pl.semaphore_signal(barrier, inc=1, device_id=partner, device_id_type=MESH_ID)
    pl.semaphore_wait(barrier, 5)

    def gather(buf, own, far, sems, to, sends, receives, arrivals):
        edge_up = Link(buf.at[own, 2], buf.at[own, 0], sems, 0, row_up, up, down)
        edge_down = Link(buf.at[own, 1], buf.at[own, 3], sems, 1, row_down, down, up)
        time_hi = Link(buf.at[own, 2], buf.at[far, 2], sems, 2, to, sends, receives)
        time_lo = Link(buf.at[own, 1], buf.at[far, 1], sems, 3, to, sends, receives)
        far_up = Link(
            buf.at[far, 2], buf.at[far, 0], sems, 4, row_up, both(up, receives), both(down, receives)
        )
        far_down = Link(
            buf.at[far, 1], buf.at[far, 3], sems, 5, row_down, both(down, receives), both(up, receives)
        )
        arrivals[0]()
        time_hi.start()
        edge_up.start()
        arrivals[1]()
        time_lo.start()
        edge_down.start()
        time_hi.wait_recv()
        far_up.start()
        time_lo.wait_recv()
        far_down.start()
        for link in (edge_up, edge_down, far_up, far_down):
            link.wait_recv()
        return [edge_up, edge_down, time_hi, time_lo, far_up, far_down]

    def columns(buf, dest, reverse):
        for t in range(3):
            for i in range(3):
                a, b = (2 - t, 2 - i) if reverse else (t, i)
                for f in range(2):
                    for r in range(2):
                        dest[pl.ds((2 * f + r) * 128, 128), pl.ds((3 * t + i) * 128, 128)] = buf[a + f, b + r]

    def hidden():
        for j in range(3):
            acc[j] = jnp.dot(
                icx[...], kin_ref[:, j].reshape(1152, 256), preferred_element_type=jnp.float32
            )

        def line(n, carry):
            at = pl.ds(pl.multiple_of(n * 128, 128), 128)
            value = joined(acc[0, at], acc[1, at], acc[2, at], False)
            hid[at] = value
            act[at] = (value / (1.0 + jnp.exp(-value))).astype(jnp.bfloat16)
            return carry

        lax.fori_loop(0, 4, line, 0)

    def upstream():
        for j in range(3):
            weights = jnp.concatenate([kout_ref[n, j] for n in range(9)], axis=1)
            acc[j] = lax.dot_general(
                icg[...], weights, (((1,), (1,)), ((), ())), preferred_element_type=jnp.float32
            )

        def line(n, carry):
            at = pl.ds(pl.multiple_of(n * 128, 128), 128)
            dgrad[at] = joined(acc[0, at], acc[1, at], acc[2, at], True)
            return carry

        lax.fori_loop(0, 4, line, 0)

    def gating():
        def line(n, carry):
            at = pl.ds(pl.multiple_of(n * 128, 128), 128)
            value = hid[at]
            sigmoid = 1.0 / (1.0 + jnp.exp(-value))
            gate[at] = (dgrad[at] * sigmoid * (1.0 + value * (1.0 - sigmoid))).astype(jnp.bfloat16)
            return carry

        lax.fori_loop(0, 4, line, 0)

    def scatter(source, reverse, sent, got, total, got_time, sems, to, sends, receives):
        seen = set()
        for t in range(3):
            for i in range(3):
                n = 3 * t + i
                if reverse:
                    product = lax.dot_general(
                        source[...], kin_ref[n].reshape(384, 256), (((1,), (1,)), ((), ())),
                        preferred_element_type=jnp.float32,
                    )
                    a, b = t, i
                else:
                    weights = jnp.concatenate([kout_ref[n, j] for j in range(3)], axis=1)
                    product = jnp.dot(source[...], weights, preferred_element_type=jnp.float32)
                    a, b = 2 - t, 2 - i
                for f in range(2):
                    for r in range(2):
                        piece = product[(2 * f + r) * 128 : (2 * f + r + 1) * 128]
                        where = (a + f, b + r)
                        if where in seen:
                            window[where] += piece
                        else:
                            window[where] = piece
                        seen.add(where)
        own, far = (2, 0) if reverse else (0, 2)

        def value(f, r):
            return joined(
                window[f, r, :, 0:128], window[f, r, :, 128:256], window[f, r, :, 256:384], reverse
            )

        links = []
        for start in (far, own):
            for f in range(2):
                sent[start + f, 0] = value(start + f, 0).astype(jnp.bfloat16)
                sent[start + f, 1] = value(start + f, 3).astype(jnp.bfloat16)
            crossing = sends if start == far else True
            span = pl.ds(start, 2)
            base = 0 if start == far else 2
            to_up = Link(
                sent.at[span, 1], got.at[span, 0], sems, base, row_up, both(up, crossing), both(down, crossing)
            )
            to_down = Link(
                sent.at[span, 0], got.at[span, 1], sems, base + 1, row_down, both(down, crossing), both(up, crossing)
            )
            to_up.start()
            to_down.start()
            links += [to_up, to_down]
        for f in range(2):
            for r in range(2):
                inner[f, r] = value(own + f, r + 1)
        links[0].wait_recv()
        links[1].wait_recv()
        for f in range(2):
            for r in range(2):
                total[f, r] = (value(far + f, r + 1) + got[far + f, r].astype(jnp.float32)).astype(jnp.bfloat16)
        in_time = Link(total, got_time, sems, 4, to, sends, receives)
        in_time.start()
        links[2].wait_recv()
        links[3].wait_recv()
        in_time.wait_recv()
        for f in range(2):
            for r in range(2):
                inner[f, r] += got[own + f, r].astype(jnp.float32) + got_time[f, r].astype(jnp.float32)
        return links + [in_time]

    own_x, far_x = pl.ds(2, 2), pl.ds(0, 2)
    own_g, far_g = pl.ds(0, 2), pl.ds(2, 2)
    seg_sems = (s_seg, r_seg)
    x_hi = Link(sect_ref.at[:, 1], xp.at[own_x, 2], seg_sems, 0, other, encodes, decodes)
    x_lo = Link(sect_ref.at[:, 0], xp.at[own_x, 1], seg_sems, 1, other, encodes, decodes)
    g_hi = Link(back_ref.at[:, 1], gp.at[own_g, 2], seg_sems, 2, other, decodes, encodes)
    g_lo = Link(back_ref.at[:, 0], gp.at[own_g, 1], seg_sems, 3, other, decodes, encodes)

    def gather_g(arrivals):
        links = gather(gp, own_g, far_g, (s_gp, r_gp), tm_earlier, earlier, later, arrivals)
        columns(gp, icg, True)
        upstream()
        for link in links:
            link.wait_send()

    @pl.when(decodes)
    def _():
        gather_g((lambda: None, lambda: None))

    links = gather(
        xp, own_x, far_x, (s_xp, r_xp), tm_later, later, earlier, (x_hi.wait_recv, x_lo.wait_recv)
    )
    columns(xp, icx, False)
    hidden()

    @pl.when(decodes)
    def _():
        gating()
        back_links = scatter(
            gate, True, sent_b, got_b, sum_b, got_zb, (s_sb, r_sb), tm_earlier, earlier, later
        )
        for r, link in ((1, g_hi), (0, g_lo)):
            for f in range(2):
                back_ref[f, r] = (gp[f, r + 1].astype(jnp.float32) + inner[f, r]).astype(jnp.bfloat16)
            link.start()
        for link in back_links:
            link.wait_send()

    links += scatter(
        act, False, sent_f, got_f, sum_f, got_zf, (s_sf, r_sf), tm_later, later, earlier
    )
    for r, link in ((1, x_hi), (0, x_lo)):
        for f in range(2):
            sect_ref[f, r] = (xp[f + 2, r + 1].astype(jnp.float32) + inner[f, r]).astype(jnp.bfloat16)
        link.start()

    @pl.when(encodes)
    def _():
        gather_g((g_hi.wait_recv, g_lo.wait_recv))
        gating()

    def widen(n, carry):
        at = pl.ds(pl.multiple_of(n * 128, 128), 128)
        for source, dest, by in ((gate, wide_e, -1), (act, wide_a, 1)):
            line = source[at].astype(jnp.float32)
            dest[at, 0:256] = shifted(line, by).astype(jnp.bfloat16)
            dest[at, 256:512] = source[at]
            dest[at, 512:768] = shifted(line, -by).astype(jnp.bfloat16)
        return carry

    lax.fori_loop(0, 4, widen, 0)
    over_cells = (((0,), (0,)), ((), ()))
    for t in range(3):
        span = pl.ds(t * 384, 384)
        product = lax.dot_general(
            icx[:, span], wide_e[...], over_cells, preferred_element_type=jnp.float32
        )
        for i in range(3):
            for j in range(3):
                fin[pl.ds((9 * t + 3 * i + j) * 128, 128)] = product[
                    i * 128 : (i + 1) * 128, j * 256 : (j + 1) * 256
                ]
        product = lax.dot_general(
            wide_a[...], icg[:, span], over_cells, preferred_element_type=jnp.float32
        )
        for i in range(3):
            for j in range(3):
                fout[pl.ds((9 * t + 3 * i + j) * 256, 256)] = product[
                    j * 256 : (j + 1) * 256, i * 128 : (i + 1) * 128
                ]

    def pack(z, carry):
        ins = fin[pl.ds(pl.multiple_of(z * 432, 432), 432)]
        outs = fout[pl.ds(pl.multiple_of(z * 864, 864), 864)]
        pad = jnp.zeros((CHUNK - 108, 128), jnp.float32)
        for k in range(16):
            part = ins[27 * k : 27 * k + 27]
            block = jnp.concatenate([part[:, :128], part[:, 128:], outs[54 * k : 54 * k + 54], pad], axis=0)
            b_ref[z, k // 8, k // 2 % 4, k % 2] = block.astype(jnp.bfloat16)
        return carry

    lax.fori_loop(0, ZS, pack, 0)
    for link in links + [x_hi, x_lo, g_hi, g_lo]:
        link.wait_send()


def front(tms, rows_count, clip, cotangent, kernel_in, kernel_out):
    whole = pl.BlockSpec(memory_space=pltpu.VMEM)
    dma = pltpu.SemaphoreType.DMA
    bf16, f32 = jnp.bfloat16, jnp.float32
    vmem = pltpu.VMEM
    tile = (128, 128)
    return pl.pallas_call(
        partial(front_kernel, tms, rows_count),
        out_shape=(
            jax.ShapeDtypeStruct((2, 2) + tile, bf16),
            jax.ShapeDtypeStruct((ZS, YS, XS, CORES, CHUNK, 128), bf16),
        ),
        in_specs=[whole] * 4,
        out_specs=(whole, whole),
        scratch_shapes=[
            vmem((2, 2) + tile, bf16),
            vmem((4, 4) + tile, bf16),
            vmem((4, 4) + tile, bf16),
            vmem((512, 1152), bf16),
            vmem((512, 1152), bf16),
            vmem((3, 512, 256), f32),
            vmem((512, 256), f32),
            vmem((512, 256), f32),
            vmem((512, 256), bf16),
            vmem((512, 256), bf16),
            vmem((4, 4, 128, 384), f32),
            vmem((2, 2) + tile, f32),
        ]
        + [vmem((4, 2) + tile, bf16), vmem((4, 2) + tile, bf16), vmem((2, 2) + tile, bf16), vmem((2, 2) + tile, bf16)] * 2
        + [
            vmem((512, 768), bf16),
            vmem((512, 768), bf16),
            vmem((3456, 256), f32),
            vmem((6912, 128), f32),
            dma((6,)), dma((6,)), dma((6,)), dma((6,)), dma((5,)), dma((5,)), dma((5,)), dma((5,)), dma((4,)), dma((4,)),
        ],
        compiler_params=pltpu.CompilerParams(
            collective_id=1, has_side_effects=True, vmem_limit_bytes=56 << 20
        ),
    )(clip, cotangent, kernel_in, kernel_out)


def on_device(tms, rows_count, input_clip, cotangent, kernel_in, kernel_out):
    sections, blocks = front(
        tms, rows_count, input_clip, cotangent,
        kernel_in.reshape(9, 3, 128, 256), kernel_out.reshape(9, 3, 256, 128),
    )
    in_sum, out_sum = reduce_scatter(blocks)
    return (sections[None], in_sum.reshape(1, -1), out_sum.reshape(1, -1))


def solution(mesh):
    in_specs = (
        P("tm", "rows", None, None),
        P("tm", "rows", None, None),
        P("segment", None, None),
        P("segment", None, None),
    )
    out_specs = (
        P("segment", "tm", "rows", None, None),
        P("segment", ("tm", "rows")),
        P("segment", ("tm", "rows")),
    )
    return jax.shard_map(
        partial(on_device, mesh.shape["tm"], mesh.shape["rows"]),
        mesh=mesh, in_specs=in_specs, out_specs=out_specs, check_vma=False,
    )
```

profile of v0, /device:TPU:2, one launch (start us, length us, event | category | flops | bytes accessed | tf_op | source)
XLA Modules:
  0.0 115.7 jit_solution(17124403725018606277)
XLA Ops:
  0.6 57.6 %shard_map.67 = (bf16[2,2,128,128]{3,2,1,0:T(8,128)(2,1)}, bf16[8,2,4,2,112,128]{5,4,3,2,1,0:T(8,128)(2,1)}) custom-call(bf16[2,2,128,128]{3,2,1,0:T(8,128)(2,1)} %x_ref.1, bf16[2,2,128,128]{3,2,1,0:T(8,128)(2,1)} %g_ref.1, bf16[9,3,128,256]{3,2,1,0:T(8,128)(2,1)} %bitcast.13, bf16[9,3,256,128]{3,2,1,0:T(8,128)(2,1)} %bitcast.14), custom_call_target="tpu_custom_call" | custom-call | tf_op jit(solution)/shard_map/pallas_call | solution.py:482
  58.2 0.0 copy-start
  58.2 2.0 %copy-done = bf16[8,2,4,2,112,128]{5,4,3,2,1,0:T(8,128)(2,1)S(1)} copy-done((bf16[8,2,4,2,112,128]{5,4,3,2,1,0:T(8,128)(2,1)S(1)}, bf16[8,2,4,2,112,128]{5,4,3,2,1,0:T(8,128)(2,1)}, u32[]{:S(2)}) %copy-start) | copy-done | bytes 3670040
  60.3 0.0 copy-start.1
  60.3 53.5 %shard_map.68 = (f32[27,256]{1,0:T(8,128)S(1)}, f32[54,128]{1,0:T(8,128)S(1)}) custom-call(bf16[8,2,4,2,112,128]{5,4,3,2,1,0:T(8,128)(2,1)S(1)} %copy-done), custom_call_target="tpu_custom_call" | custom-call | tf_op jit(solution)/shard_map/pallas_call | solution.py:134
  113.8 0.6 copy.10
  114.4 0.6 copy.7
  115.0 0.0 copy-done.1
  115.1 0.7 copy.12
Async XLA Ops:
  58.2 2.0 %copy-start = (bf16[8,2,4,2,112,128]{5,4,3,2,1,0:T(8,128)(2,1)S(1)}, bf16[8,2,4,2,112,128]{5,4,3,2,1,0:T(8,128)(2,1)}, u32[]{:S(2)}) copy-start(bf16[8,2,4,2,112,128]{5,4,3,2,1,0:T(8,128)(2,1)} %get-tuple-element.8.b_ref) | copy-start | bytes 11010052
  60.3 54.8 %copy-start.1 = (bf16[2,2,128,128]{3,2,1,0:T(8,128)(2,1)S(1)}, bf16[2,2,128,128]{3,2,1,0:T(8,128)(2,1)}, u32[]{:S(2)}) copy-start(bf16[2,2,128,128]{3,2,1,0:T(8,128)(2,1)} %get-tuple-element.7) | copy-start | bytes 393220
where the time goes:
time: 116 us
  Pallas kernels  111 us (96%)
  local copies, waits for them, and re-layouts  3.97 us (3%)
    pallas_call x1, Pallas kernels, front(): pl.pallas_call(partial(front_kernel, tms, rows_count), out_shape=(jax.Sha...  57.6 us
    pallas_call x1, Pallas kernels, reduce_scatter(): pl.pallas_call(reduce_scatter_kernel, out_shape=(jax.ShapeDtypeStruct((27...  53.5 us
    unnamed x7, local copies, waits for them, and re-layouts  3.97 us

commit v1 on v0

--- a/solution.py
+++ b/solution.py
@@ -12,148 +12,7 @@
 CHUNK = 112
 
 
-def reduce_scatter_kernel(
-    b_ref, in_ref, out_ref, got_core, half, got_x, mine, quarter, got_z, last, got_y,
-    send_core, recv_core, send_x, recv_x, send_z, recv_z, send_y, recv_y,
-):
-    row = lax.axis_index("rows")
-    tm = lax.axis_index("tm")
-    core = lax.rem(row, 2)
-    at_x = lax.rem(row // 2, 4)
-    at_y = row // 8
-
-    def row_of(y, x, c):
-        return y * 8 + x * 2 + c
-
-    def x_at(offset):
-        return lax.rem(at_x + offset, XS)
-
-    def z_at(offset):
-        return lax.rem(tm + offset, ZS)
-
-    sibling = {"rows": row_of(at_y, at_x, 1 - core)}
-    across_y = {"rows": row_of(1 - at_y, at_x, core)}
-    barrier = pltpu.get_barrier_semaphore()
-    partners = [sibling, across_y]
-    partners += [{"rows": row_of(at_y, x_at(o), core)} for o in range(1, XS)]
-    partners += [{"tm": z_at(p)} for p in range(1, ZS)]
-    for partner in partners:
-        pl.semaphore_signal(barrier, inc=1, device_id=partner, device_id_type=MESH_ID)
-    pl.semaphore_wait(barrier, len(partners))
-
-    order = (2, 1, 3, 0)
-    core_copies = {}
-    for o in order:
-        copy = pltpu.make_async_remote_copy(
-            src_ref=b_ref.at[:, :, x_at(o), 1 - core],
-            dst_ref=got_core.at[o],
-            send_sem=send_core.at[o],
-            recv_sem=recv_core.at[o],
-            device_id=sibling,
-            device_id_type=MESH_ID,
-        )
-        copy.start()
-        core_copies[o] = copy
-    x_copies = []
-    for o in order:
-        core_copies[o].wait_recv()
-        x = x_at(o)
-
-        def add_core(z, carry, o=o, x=x):
-            total = b_ref[z, :, x, core].astype(jnp.float32) + got_core[o, z].astype(jnp.float32)
-            if o == 0:
-                mine[z] = total
-            else:
-                half[o, z] = total.astype(jnp.bfloat16)
-            return carry
-
-        lax.fori_loop(0, ZS, add_core, 0)
-        if o:
-            copy = pltpu.make_async_remote_copy(
-                src_ref=half.at[o],
-                dst_ref=got_x.at[o],
-                send_sem=send_x.at[o],
-                recv_sem=recv_x.at[o],
-                device_id={"rows": row_of(at_y, x, core)},
-                device_id_type=MESH_ID,
-            )
-            copy.start()
-            x_copies.append(copy)
-    for copy in x_copies:
-        copy.wait_recv()
-    z_copies = []
-    for p in (4, 3, 5, 2, 6, 1, 7, 0):
-        z = z_at(p)
-        total = mine[z]
-        for o in range(1, XS):
-            total = total + got_x[o, z].astype(jnp.float32)
-        if p == 0:
-            mine[z] = total
-        else:
-            quarter[p] = total.astype(jnp.bfloat16)
-            copy = pltpu.make_async_remote_copy(
-                src_ref=quarter.at[p],
-                dst_ref=got_z.at[p],
-                send_sem=send_z.at[p],
-                recv_sem=recv_z.at[p],
-                device_id={"tm": z},
-                device_id_type=MESH_ID,
-            )
-            copy.start()
-            z_copies.append(copy)
-    for copy in z_copies:
-        copy.wait_recv()
-    for side in range(YS):
-        total = mine[tm, side]
-        for p in range(1, ZS):
-            total = total + got_z[p, side].astype(jnp.float32)
-        mine[tm, side] = total
-    last[...] = mine[tm, 1 - at_y].astype(jnp.bfloat16)
-    copy = pltpu.make_async_remote_copy(
-        src_ref=last,
-        dst_ref=got_y,
-        send_sem=send_y,
-        recv_sem=recv_y,
-        device_id=across_y,
-        device_id_type=MESH_ID,
-    )
-    copy.start()
-    copy.wait_recv()
-    total = mine[tm, at_y] + got_y[...].astype(jnp.float32)
-    in_ref[:, 0:128] = total[0:27]
-    in_ref[:, 128:256] = total[27:54]
-    out_ref[...] = total[54:108]
-    for copy in [core_copies[o] for o in order] + x_copies + z_copies + [copy]:
-        copy.wait_send()
-
-
-def reduce_scatter(blocks):
-    whole = pl.BlockSpec(memory_space=pltpu.VMEM)
-    tile = (CHUNK, 128)
-    dma = pltpu.SemaphoreType.DMA
-    return pl.pallas_call(
-        reduce_scatter_kernel,
-        out_shape=(
-            jax.ShapeDtypeStruct((27, 256), jnp.float32),
-            jax.ShapeDtypeStruct((54, 128), jnp.float32),
-        ),
-        in_specs=[whole],
-        out_specs=(whole, whole),
-        scratch_shapes=[
-            pltpu.VMEM((XS, ZS, YS) + tile, jnp.bfloat16),
-            pltpu.VMEM((XS, ZS, YS) + tile, jnp.bfloat16),
-            pltpu.VMEM((XS, ZS, YS) + tile, jnp.bfloat16),
-            pltpu.VMEM((ZS, YS) + tile, jnp.float32),
-            pltpu.VMEM((ZS, YS) + tile, jnp.bfloat16),
-            pltpu.VMEM((ZS, YS) + tile, jnp.bfloat16),
-            pltpu.VMEM(tile, jnp.bfloat16),
-            pltpu.VMEM(tile, jnp.bfloat16),
-            dma((XS,)), dma((XS,)), dma((XS,)), dma((XS,)), dma((ZS,)), dma((ZS,)), dma, dma,
-        ],
-        compiler_params=pltpu.CompilerParams(
-            collective_id=0, has_side_effects=True, vmem_limit_bytes=40 << 20
-        ),
-    )(blocks)
+TOP = 64
 
 
 def shifted(line, by):
@@ -199,11 +58,12 @@
 
 
 def front_kernel(
-    tms, rows_count, x_ref, g_ref, kin_ref, kout_ref, sect_ref, b_ref,
-    back_ref, xp, gp, icx, icg, acc, hid, dgrad, act, gate, window, inner,
+    tms, rows_count, x_ref, g_ref, kin_hbm, kout_hbm, sect_ref, in_ref, out_ref,
+    kin_ref, kout_ref, s_load, back_ref, xp, gp, icx, icg, acc, hid, dgrad, act, gate, window, inner,
     sent_f, got_f, sum_f, got_zf, sent_b, got_b, sum_b, got_zb,
     wide_e, wide_a, fin, fout,
     s_xp, r_xp, s_gp, r_gp, s_sf, r_sf, s_sb, r_sb, s_seg, r_seg,
+    *reduce_refs,
 ):
     seg = lax.axis_index("segment")
     tm = lax.axis_index("tm")
@@ -218,6 +78,19 @@
     tm_earlier = {"tm": lax.rem(tm + tms - 1, tms)}
     other = {"segment": 1 - seg}
     both = jnp.logical_and
+    core, at_x, at_y = lax.rem(row, 2), lax.rem(row // 2, XS), row // 8
+
+    def x_at(offset):
+        return lax.rem(at_x + offset, XS)
+
+    sibling = {"rows": at_y * 8 + at_x * 2 + 1 - core}
+    across_y = {"rows": (1 - at_y) * 8 + at_x * 2 + core}
+    across_x = [{"rows": at_y * 8 + x_at(o) * 2 + core} for o in range(1, XS)]
+    in_time = [{"tm": lax.rem(tm + p, ZS)} for p in range(1, ZS)]
+    load_in = pltpu.make_async_copy(kin_hbm, kin_ref, s_load.at[0])
+    load_out = pltpu.make_async_copy(kout_hbm, kout_ref, s_load.at[1])
+    load_in.start()
+    load_out.start()
 
     xp[...] = jnp.zeros_like(xp)
     gp[...] = jnp.zeros_like(gp)
@@ -235,9 +108,10 @@
         gp[0:2, 1:3] = g_ref[...]
 
     barrier = pltpu.get_barrier_semaphore()
-    for partner in (row_up, row_down, tm_later, tm_earlier, other):
+    partners = [row_up, row_down, other, sibling, across_y] + across_x + in_time
+    for partner in partners:
         pl.semaphore_signal(barrier, inc=1, device_id=partner, device_id_type=MESH_ID)
-    pl.semaphore_wait(barrier, 5)
+    pl.semaphore_wait(barrier, len(partners))
 
     def gather(buf, own, far, sems, to, sends, receives, arrivals):
         edge_up = Link(buf.at[own, 2], buf.at[own, 0], sems, 0, row_up, up, down)
@@ -367,15 +241,15 @@
         for f in range(2):
             for r in range(2):
                 total[f, r] = (value(far + f, r + 1) + got[far + f, r].astype(jnp.float32)).astype(jnp.bfloat16)
-        in_time = Link(total, got_time, sems, 4, to, sends, receives)
-        in_time.start()
+        ahead = Link(total, got_time, sems, 4, to, sends, receives)
+        ahead.start()
         links[2].wait_recv()
         links[3].wait_recv()
-        in_time.wait_recv()
+        ahead.wait_recv()
         for f in range(2):
             for r in range(2):
                 inner[f, r] += got[own + f, r].astype(jnp.float32) + got_time[f, r].astype(jnp.float32)
-        return links + [in_time]
+        return links + [ahead]
 
     own_x, far_x = pl.ds(2, 2), pl.ds(0, 2)
     own_g, far_g = pl.ds(0, 2), pl.ds(2, 2)
@@ -391,6 +265,9 @@
         upstream()
         for link in links:
             link.wait_send()
+
+    load_in.wait()
+    load_out.wait()
 
     @pl.when(decodes)
     def _():
@@ -458,19 +335,137 @@
                     j * 256 : (j + 1) * 256, i * 128 : (i + 1) * 128
                 ]
 
-    def pack(z, carry):
-        ins = fin[pl.ds(pl.multiple_of(z * 432, 432), 432)]
-        outs = fout[pl.ds(pl.multiple_of(z * 864, 864), 864)]
-        pad = jnp.zeros((CHUNK - 108, 128), jnp.float32)
+    reduce_scatter(
+        fin, fout, in_ref, out_ref, tm, core, at_y, x_at, sibling, across_y, *reduce_refs
+    )
+    for link in links + [x_hi, x_lo, g_hi, g_lo]:
+        link.wait_send()
+
+
+def reduce_scatter(
+    fin, fout, in_ref, out_ref, tm, core, at_y, x_at, sibling, across_y,
+    blocks, got_core, half_a, got_a, half_c, got_c, next_a, got_a2, next_c, got_c2,
+    own_a, own_c, last, got_z,
+    s_core, r_core, s_a, r_a, s_c, r_c, s_a2, r_a2, s_c2, r_c2, s_z, r_z,
+):
+    f32, bf16 = jnp.float32, jnp.bfloat16
+
+    def send(src, dst, send_sem, recv_sem, device):
+        copy = pltpu.make_async_remote_copy(
+            src_ref=src, dst_ref=dst, send_sem=send_sem, recv_sem=recv_sem,
+            device_id=device, device_id_type=MESH_ID,
+        )
+        copy.start()
+        return copy
+
+    def x_device(o):
+        return {"rows": at_y * 8 + x_at(o) * 2 + core}
+
+    def core_copy(q):
+        return pltpu.make_async_remote_copy(
+            src_ref=blocks.at[q, :, :, 1 - core], dst_ref=got_core.at[q],
+            send_sem=s_core.at[q], recv_sem=r_core.at[q],
+            device_id=sibling, device_id_type=MESH_ID,
+        )
+
+    def pack(q, carry):
+        odd = lax.rem(q, 2)
+        offset = 4 + (1 - odd) * (q // 2) - odd * ((q + 1) // 2)
+        z = lax.rem(tm + offset, ZS)
+        ins = fin[pl.ds(pl.multiple_of(z * 432, 16), 432)]
+        outs = fout[pl.ds(pl.multiple_of(z * 864, 16), 864)]
+        pad = jnp.zeros((CHUNK - 108, 128), f32)
         for k in range(16):
             part = ins[27 * k : 27 * k + 27]
             block = jnp.concatenate([part[:, :128], part[:, 128:], outs[54 * k : 54 * k + 54], pad], axis=0)
-            b_ref[z, k // 8, k // 2 % 4, k % 2] = block.astype(jnp.bfloat16)
+            blocks[q, k // 8, k // 2 % 4, k % 2] = block.astype(bf16)
+        core_copy(q).start()
         return carry
 
     lax.fori_loop(0, ZS, pack, 0)
-    for link in links + [x_hi, x_lo, g_hi, g_lo]:
-        link.wait_send()
+    copies = []
+    firsts = []
+    for h in range(2):
+
+        def add_core(n, carry, h=h):
+            q = 4 * h + n
+            core_copy(q).wait_recv()
+            for o in range(XS):
+                for y in range(YS):
+                    x = x_at(o)
+                    side = lax.rem(at_y + y, 2)
+                    total = blocks[q, side, x, core].astype(f32) + got_core[q, side, x].astype(f32)
+                    half_a[h, o, n, y] = total[0:TOP].astype(bf16)
+                    half_c[h, y, n, o] = total[TOP:CHUNK].astype(bf16)
+            return carry
+
+        lax.fori_loop(0, 4, add_core, 0)
+        sent = []
+        for o in (2, 1, 3):
+            sent.append(send(half_a.at[h, o], got_a.at[h, o], s_a.at[h, o], r_a.at[h, o], x_device(o)))
+        sent.append(send(half_c.at[h, 1], got_c.at[h], s_c.at[h], r_c.at[h], across_y))
+        firsts.append(sent)
+        copies += sent
+    seconds = []
+    for h in range(2):
+        for copy in firsts[h]:
+            copy.wait_recv()
+
+        def add_first(n, carry, h=h):
+            for y in range(YS):
+                total = half_a[h, 0, n, y].astype(f32)
+                for o in range(1, XS):
+                    total = total + got_a[h, o, n, y].astype(f32)
+                if y == 0:
+                    own_a[h, n] = total
+                else:
+                    next_a[h, n] = total.astype(bf16)
+            for o in range(XS):
+                total = half_c[h, 0, n, o].astype(f32) + got_c[h, n, o].astype(f32)
+                if o == 0:
+                    own_c[h, n] = total
+                else:
+                    next_c[h, o, n] = total.astype(bf16)
+            return carry
+
+        lax.fori_loop(0, 4, add_first, 0)
+        sent = [send(next_a.at[h], got_a2.at[h], s_a2.at[h], r_a2.at[h], across_y)]
+        for o in (2, 1, 3):
+            sent.append(send(next_c.at[h, o], got_c2.at[h, o], s_c2.at[h, o], r_c2.at[h, o], x_device(o)))
+        seconds.append(sent)
+        copies += sent
+    thirds = []
+    total = None
+    for h in range(2):
+        for copy in seconds[h]:
+            copy.wait_recv()
+        for n in range(4):
+            q = 4 * h + n
+            top = own_a[h, n] + got_a2[h, n].astype(f32)
+            low = own_c[h, n]
+            for o in range(1, XS):
+                low = low + got_c2[h, o, n].astype(f32)
+            total = jnp.concatenate([top, low], axis=0)
+            if q < ZS - 1:
+                offset = 4 + q // 2 if q % 2 == 0 else 4 - (q + 1) // 2
+                last[q] = total.astype(bf16)
+                thirds.append(
+                    send(last.at[q], got_z.at[q], s_z.at[q], r_z.at[q], {"tm": lax.rem(tm + offset, ZS)})
+                )
+    for q, copy in enumerate(thirds):
+        copy.wait_recv()
+        total = total + got_z[q].astype(f32)
+    in_ref[:, 0:128] = total[0:27]
+    in_ref[:, 128:256] = total[27:54]
+    out_ref[...] = total[54:108]
+    for copy in copies + thirds:
+        copy.wait_send()
+
+    def drain(q, carry):
+        core_copy(q).wait_send()
+        return carry
+
+    lax.fori_loop(0, ZS, drain, 0)
 
 
 def front(tms, rows_count, clip, cotangent, kernel_in, kernel_out):
@@ -483,11 +478,15 @@
         partial(front_kernel, tms, rows_count),
         out_shape=(
             jax.ShapeDtypeStruct((2, 2) + tile, bf16),
-            jax.ShapeDtypeStruct((ZS, YS, XS, CORES, CHUNK, 128), bf16),
+            jax.ShapeDtypeStruct((27, 256), f32),
+            jax.ShapeDtypeStruct((54, 128), f32),
         ),
-        in_specs=[whole] * 4,
-        out_specs=(whole, whole),
+        in_specs=[whole, whole, pl.BlockSpec(memory_space=pl.ANY), pl.BlockSpec(memory_space=pl.ANY)],
+        out_specs=(whole, whole, whole),
         scratch_shapes=[
+            vmem((9, 3, 128, 256), bf16),
+            vmem((9, 3, 256, 128), bf16),
+            dma((2,)),
             vmem((2, 2) + tile, bf16),
             vmem((4, 4) + tile, bf16),
             vmem((4, 4) + tile, bf16),
@@ -508,6 +507,22 @@
             vmem((3456, 256), f32),
             vmem((6912, 128), f32),
             dma((6,)), dma((6,)), dma((6,)), dma((6,)), dma((5,)), dma((5,)), dma((5,)), dma((5,)), dma((4,)), dma((4,)),
+            vmem((ZS, YS, XS, CORES, CHUNK, 128), bf16),
+            vmem((ZS, YS, XS, CHUNK, 128), bf16),
+            vmem((2, XS, 4, YS, TOP, 128), bf16),
+            vmem((2, XS, 4, YS, TOP, 128), bf16),
+            vmem((2, YS, 4, XS, CHUNK - TOP, 128), bf16),
+            vmem((2, 4, XS, CHUNK - TOP, 128), bf16),
+            vmem((2, 4, TOP, 128), bf16),
+            vmem((2, 4, TOP, 128), bf16),
+            vmem((2, XS, 4, CHUNK - TOP, 128), bf16),
+            vmem((2, XS, 4, CHUNK - TOP, 128), bf16),
+            vmem((2, 4, TOP, 128), f32),
+            vmem((2, 4, CHUNK - TOP, 128), f32),
+            vmem((ZS, CHUNK, 128), bf16),
+            vmem((ZS, CHUNK, 128), bf16),
+            dma((ZS,)), dma((ZS,)), dma((2, XS)), dma((2, XS)), dma((2,)), dma((2,)),
+            dma((2,)), dma((2,)), dma((2, XS)), dma((2, XS)), dma((ZS,)), dma((ZS,)),
         ],
         compiler_params=pltpu.CompilerParams(
             collective_id=1, has_side_effects=True, vmem_limit_bytes=56 << 20
@@ -516,11 +531,10 @@
 
 
 def on_device(tms, rows_count, input_clip, cotangent, kernel_in, kernel_out):
-    sections, blocks = front(
+    sections, in_sum, out_sum = front(
         tms, rows_count, input_clip, cotangent,
         kernel_in.reshape(9, 3, 128, 256), kernel_out.reshape(9, 3, 256, 128),
     )
-    in_sum, out_sum = reduce_scatter(blocks)
     return (sections[None], in_sum.reshape(1, -1), out_sum.reshape(1, -1))
 
 

time: 116 us -> 102 us (0.88)
  Pallas kernels: 111 us -> 95.9 us
    pallas_call x1 -> x0, Pallas kernels: 53.5 us -> none  [reduce_scatter(): pl.pallas_call(reduce_scatter_kernel, out_shape=(jax.ShapeDtypeStruct((27...]
    pallas_call x1, Pallas kernels: 57.6 us -> 95.9 us  [front(): pl.pallas_call(partial(front_kernel, tms, rows_count), out_shape=(jax.Sha...]
    unnamed x7 -> x3, local copies, waits for them, and re-layouts: 3.97 us -> 4.35 us
where the time goes in v1:
time: 102 us; the launch traced here: 101 us
  Pallas kernels  95.9 us (94%)
  local copies, waits for them, and re-layouts  4.35 us (4%)
    pallas_call x1, Pallas kernels, front(): pl.pallas_call(partial(front_kernel, tms, rows_count), out_shape=(jax.Sha...  95.9 us
    unnamed x3, local copies, waits for them, and re-layouts  4.35 us

profile of v1, /device:TPU:2, one launch (start us, length us, event | category | flops | bytes accessed | tf_op | source)
XLA Modules:
  0.0 100.9 jit_solution(18123608536984408971)
XLA Ops:
  0.6 95.9 %shard_map.67 = (bf16[2,2,128,128]{3,2,1,0:T(8,128)(2,1)}, f32[27,256]{1,0:T(8,128)}, f32[54,128]{1,0:T(8,128)}) custom-call(bf16[2,2,128,128]{3,2,1,0:T(8,128)(2,1)} %x_ref.1, bf16[2,2,128,128]{3,2,1,0:T(8,128)(2,1)} %g_ref.1, bf16[9,3,128,256]{3,2,1,0:T(8,128)(2,1)} %bitcast.11, bf16[9,3,256,128]{3,2,1,0:T(8,128)(2,1)} %bitcast.12), custom_call_target="tpu_custom_call" | custom-call | tf_op jit(solution)/shard_map/pallas_call | solution.py:477
  96.5 1.4 %copy.7 = f32[1,1,27,256]{3,1,2,0:T(1,128)} copy(f32[1,1,27,256]{3,2,1,0:T(8,128)} %bitcast.14) | data formatting | bytes 55296
  97.9 1.4 %copy.10 = f32[1,1,54,128]{3,1,2,0:T(1,128)} copy(f32[1,1,54,128]{3,2,1,0:T(8,128)} %bitcast.15) | data formatting | bytes 55296
  99.3 1.6 %copy.12 = bf16[1,2,2,128,128]{4,3,2,1,0:T(8,128)(2,1)} copy(bf16[1,2,2,128,128]{4,3,2,1,0:T(8,128)(2,1)} %bitcast.13) | data formatting | bytes 262144

commit v2 on v1

--- a/solution.py
+++ b/solution.py
@@ -13,6 +13,8 @@
 
 
 TOP = 64
+EARLY, LATE = (6, 7, 8, 1, 4), (0, 2, 3, 5)
+PLACES = EARLY + LATE
 
 
 def shifted(line, by):
@@ -70,22 +72,23 @@
     row = lax.axis_index("rows")
     encodes = seg == 0
     decodes = seg == 1
-    up, down = row + 1 < rows_count, row > 0
     later, earlier = tm + 1 < tms, tm > 0
-    row_up = {"rows": lax.rem(row + 1, rows_count)}
-    row_down = {"rows": lax.rem(row + rows_count - 1, rows_count)}
     tm_later = {"tm": lax.rem(tm + 1, tms)}
     tm_earlier = {"tm": lax.rem(tm + tms - 1, tms)}
     other = {"segment": 1 - seg}
     both = jnp.logical_and
-    core, at_x, at_y = lax.rem(row, 2), lax.rem(row // 2, XS), row // 8
+    core, at_x, at_y = lax.rem(row, 2), lax.rem(row // 2, XS), row // (XS * CORES)
+
+    step = 2 * core - 1
+    crosses = both(row + step >= 0, row + step < rows_count)
+    across = {"rows": lax.rem(row + step + rows_count, rows_count)}
 
     def x_at(offset):
         return lax.rem(at_x + offset, XS)
 
-    sibling = {"rows": at_y * 8 + at_x * 2 + 1 - core}
-    across_y = {"rows": (1 - at_y) * 8 + at_x * 2 + core}
-    across_x = [{"rows": at_y * 8 + x_at(o) * 2 + core} for o in range(1, XS)]
+    sibling = {"rows": at_y * (XS * CORES) + at_x * 2 + 1 - core}
+    across_y = {"rows": (1 - at_y) * (XS * CORES) + at_x * 2 + core}
+    across_x = [{"rows": at_y * (XS * CORES) + x_at(o) * 2 + core} for o in range(1, XS)]
     in_time = [{"tm": lax.rem(tm + p, ZS)} for p in range(1, ZS)]
     load_in = pltpu.make_async_copy(kin_hbm, kin_ref, s_load.at[0])
     load_out = pltpu.make_async_copy(kout_hbm, kout_ref, s_load.at[1])
@@ -108,50 +111,75 @@
         gp[0:2, 1:3] = g_ref[...]
 
     barrier = pltpu.get_barrier_semaphore()
-    partners = [row_up, row_down, other, sibling, across_y] + across_x + in_time
+    partners = [across, other, sibling, across_y] + across_x + in_time
     for partner in partners:
         pl.semaphore_signal(barrier, inc=1, device_id=partner, device_id_type=MESH_ID)
     pl.semaphore_wait(barrier, len(partners))
 
-    def gather(buf, own, far, sems, to, sends, receives, arrivals):
-        edge_up = Link(buf.at[own, 2], buf.at[own, 0], sems, 0, row_up, up, down)
-        edge_down = Link(buf.at[own, 1], buf.at[own, 3], sems, 1, row_down, down, up)
-        time_hi = Link(buf.at[own, 2], buf.at[far, 2], sems, 2, to, sends, receives)
-        time_lo = Link(buf.at[own, 1], buf.at[far, 1], sems, 3, to, sends, receives)
-        far_up = Link(
-            buf.at[far, 2], buf.at[far, 0], sems, 4, row_up, both(up, receives), both(down, receives)
-        )
-        far_down = Link(
-            buf.at[far, 1], buf.at[far, 3], sems, 5, row_down, both(down, receives), both(up, receives)
-        )
-        arrivals[0]()
-        time_hi.start()
-        edge_up.start()
-        arrivals[1]()
-        time_lo.start()
-        edge_down.start()
-        time_hi.wait_recv()
-        far_up.start()
-        time_lo.wait_recv()
-        far_down.start()
-        for link in (edge_up, edge_down, far_up, far_down):
+    inner_rows = (1 + core, 2 - core)
+    row_devices = (across, sibling)
+    edge_slots = (3 * (1 - core), 3 * core)
+    outer_rows = (3 * core, 3 * (1 - core))
+    row_exists = (crosses, True)
+
+    def gather(buf, own, far, sems, to, sends, receives, arrivals, order, early):
+        edges, times, fars = [], [], []
+        for k in range(2):
+            device, slot = row_devices[k], edge_slots[k]
+            edges.append(
+                Link(buf.at[own, inner_rows[k]], buf.at[own, slot], sems, k, device, row_exists[k], row_exists[k])
+            )
+            times.append(
+                Link(buf.at[own, inner_rows[k]], buf.at[far, inner_rows[k]], sems, 2 + k, to, sends, receives)
+            )
+            crossing = both(row_exists[k], receives)
+            fars.append(
+                Link(buf.at[far, inner_rows[k]], buf.at[far, slot], sems, 4 + k, device, crossing, crossing)
+            )
+        for k in order:
+            arrivals[k]()
+            times[k].start()
+            edges[k].start()
+        for k in order:
+            times[k].wait_recv()
+            fars[k].start()
+        for link in edges:
             link.wait_recv()
-        return [edge_up, edge_down, time_hi, time_lo, far_up, far_down]
-
-    def columns(buf, dest, reverse):
-        for t in range(3):
-            for i in range(3):
-                a, b = (2 - t, 2 - i) if reverse else (t, i)
-                for f in range(2):
-                    for r in range(2):
-                        dest[pl.ds((2 * f + r) * 128, 128), pl.ds((3 * t + i) * 128, 128)] = buf[a + f, b + r]
-
-    def hidden():
+        early()
+        for link in fars:
+            link.wait_recv()
+        return edges + times + fars
+
+    def columns(buf, dest, reverse, taps):
+        for n in taps:
+            t, i = n // 3, n % 3
+            a, b = (2 - t, 2 - i) if reverse else (t, i)
+            for f in range(2):
+                for r in range(2):
+                    dest[pl.ds((2 * f + r) * 128, 128), pl.ds(PLACES.index(n) * 128, 128)] = buf[a + f, b + r]
+
+    def conv_part(taps, source, weights_of, contract, add):
+        span = pl.ds(PLACES.index(taps[0]) * 128, len(taps) * 128)
         for j in range(3):
-            acc[j] = jnp.dot(
-                icx[...], kin_ref[:, j].reshape(1152, 256), preferred_element_type=jnp.float32
+            product = lax.dot_general(
+                source[:, span], weights_of(taps, j), (((1,), (contract,)), ((), ())),
+                preferred_element_type=jnp.float32,
             )
-
+            acc[j] = acc[j] + product if add else product
+
+    def hidden_part(taps, add):
+        columns(xp, icx, False, taps)
+        conv_part(
+            taps, icx, lambda ns, j: jnp.concatenate([kin_ref[n, j] for n in ns], axis=0), 0, add
+        )
+
+    def upstream_part(taps, add):
+        columns(gp, icg, True, taps)
+        conv_part(
+            taps, icg, lambda ns, j: jnp.concatenate([kout_ref[n, j] for n in ns], axis=1), 1, add
+        )
+
+    def activate():
         def line(n, carry):
             at = pl.ds(pl.multiple_of(n * 128, 128), 128)
             value = joined(acc[0, at], acc[1, at], acc[2, at], False)
@@ -161,13 +189,7 @@
 
         lax.fori_loop(0, 4, line, 0)
 
-    def upstream():
-        for j in range(3):
-            weights = jnp.concatenate([kout_ref[n, j] for n in range(9)], axis=1)
-            acc[j] = lax.dot_general(
-                icg[...], weights, (((1,), (1,)), ((), ())), preferred_element_type=jnp.float32
-            )
-
+    def keep_upstream():
         def line(n, carry):
             at = pl.ds(pl.multiple_of(n * 128, 128), 128)
             dgrad[at] = joined(acc[0, at], acc[1, at], acc[2, at], True)
@@ -185,9 +207,11 @@
 
         lax.fori_loop(0, 4, line, 0)
 
-    def scatter(source, reverse, sent, got, total, got_time, sems, to, sends, receives):
+    def scatter(source, reverse, sent, got, total, got_time, sems, to, sends, receives, finish):
         seen = set()
-        for t in range(3):
+        own, far = (2, 0) if reverse else (0, 2)
+
+        def products(t):
             for i in range(3):
                 n = 3 * t + i
                 if reverse:
@@ -209,100 +233,124 @@
                         else:
                             window[where] = piece
                         seen.add(where)
-        own, far = (2, 0) if reverse else (0, 2)
 
         def value(f, r):
             return joined(
                 window[f, r, :, 0:128], window[f, r, :, 128:256], window[f, r, :, 256:384], reverse
             )
 
-        links = []
-        for start in (far, own):
+        def send_edges(start, base, exists):
+            links = []
+            for k in range(2):
+                for f in range(2):
+                    sent[k, start + f] = value(start + f, outer_rows[k]).astype(jnp.bfloat16)
+                span = pl.ds(start, 2)
+                goes = both(row_exists[k], exists)
+                link = Link(sent.at[k, span], got.at[k, span], sems, base + k, row_devices[k], goes, goes)
+                link.start()
+                links.append(link)
+            return links
+
+        products(0)
+        products(1)
+        far_links = send_edges(far, 0, sends)
+        products(2)
+        own_links = send_edges(own, 2, True)
+        time_links = []
+        for k in (1, 0):
+            far_links[k].wait_recv()
             for f in range(2):
-                sent[start + f, 0] = value(start + f, 0).astype(jnp.bfloat16)
-                sent[start + f, 1] = value(start + f, 3).astype(jnp.bfloat16)
-            crossing = sends if start == far else True
-            span = pl.ds(start, 2)
-            base = 0 if start == far else 2
-            to_up = Link(
-                sent.at[span, 1], got.at[span, 0], sems, base, row_up, both(up, crossing), both(down, crossing)
+                total[k, f] = (
+                    value(far + f, inner_rows[k]) + got[k, far + f].astype(jnp.float32)
+                ).astype(jnp.bfloat16)
+            link = Link(total.at[k], got_time.at[k], sems, 4 + k, to, sends, receives)
+            link.start()
+            time_links.append(link)
+        for k, link in zip((1, 0), time_links):
+            for f in range(2):
+                inner[k, f] = value(own + f, inner_rows[k])
+            own_links[k].wait_recv()
+            link.wait_recv()
+            finish(
+                k,
+                [
+                    inner[k, f] + got[k, own + f].astype(jnp.float32) + got_time[k, f].astype(jnp.float32)
+                    for f in range(2)
+                ],
             )
-            to_down = Link(
-                sent.at[span, 0], got.at[span, 1], sems, base + 1, row_down, both(down, crossing), both(up, crossing)
-            )
-            to_up.start()
-            to_down.start()
-            links += [to_up, to_down]
-        for f in range(2):
-            for r in range(2):
-                inner[f, r] = value(own + f, r + 1)
-        links[0].wait_recv()
-        links[1].wait_recv()
-        for f in range(2):
-            for r in range(2):
-                total[f, r] = (value(far + f, r + 1) + got[far + f, r].astype(jnp.float32)).astype(jnp.bfloat16)
-        ahead = Link(total, got_time, sems, 4, to, sends, receives)
-        ahead.start()
-        links[2].wait_recv()
-        links[3].wait_recv()
-        ahead.wait_recv()
-        for f in range(2):
-            for r in range(2):
-                inner[f, r] += got[own + f, r].astype(jnp.float32) + got_time[f, r].astype(jnp.float32)
-        return links + [ahead]
+        return far_links + own_links + time_links
 
     own_x, far_x = pl.ds(2, 2), pl.ds(0, 2)
     own_g, far_g = pl.ds(0, 2), pl.ds(2, 2)
     seg_sems = (s_seg, r_seg)
-    x_hi = Link(sect_ref.at[:, 1], xp.at[own_x, 2], seg_sems, 0, other, encodes, decodes)
-    x_lo = Link(sect_ref.at[:, 0], xp.at[own_x, 1], seg_sems, 1, other, encodes, decodes)
-    g_hi = Link(back_ref.at[:, 1], gp.at[own_g, 2], seg_sems, 2, other, decodes, encodes)
-    g_lo = Link(back_ref.at[:, 0], gp.at[own_g, 1], seg_sems, 3, other, decodes, encodes)
-
-    def gather_g(arrivals):
-        links = gather(gp, own_g, far_g, (s_gp, r_gp), tm_earlier, earlier, later, arrivals)
-        columns(gp, icg, True)
-        upstream()
+    x_links, g_links = [], []
+    for k in range(2):
+        place = inner_rows[k]
+        x_links.append(
+            Link(sect_ref.at[:, place - 1], xp.at[own_x, place], seg_sems, k, other, encodes, decodes)
+        )
+        g_links.append(
+            Link(back_ref.at[:, place - 1], gp.at[own_g, place], seg_sems, 2 + k, other, decodes, encodes)
+        )
+
+    def gather_g(arrivals, order):
+        links = gather(
+            gp, own_g, far_g, (s_gp, r_gp), tm_earlier, earlier, later, arrivals, order,
+            lambda: upstream_part(EARLY, False),
+        )
+        upstream_part(LATE, True)
+        keep_upstream()
         for link in links:
             link.wait_send()
 
+    def gather_x(arrivals, order):
+        links = gather(
+            xp, own_x, far_x, (s_xp, r_xp), tm_later, later, earlier, arrivals, order,
+            lambda: hidden_part(EARLY, False),
+        )
+        hidden_part(LATE, True)
+        activate()
+        for link in links:
+            link.wait_send()
+
+    def finish_x(k, sums):
+        place = inner_rows[k]
+        for f in range(2):
+            sect_ref[f, place - 1] = (xp[f + 2, place].astype(jnp.float32) + sums[f]).astype(jnp.bfloat16)
+        x_links[k].start()
+
+    def finish_g(k, sums):
+        place = inner_rows[k]
+        for f in range(2):
+            back_ref[f, place - 1] = (gp[f, place].astype(jnp.float32) + sums[f]).astype(jnp.bfloat16)
+        g_links[k].start()
+
+    at_once = (lambda: None, lambda: None)
     load_in.wait()
     load_out.wait()
 
+    @pl.when(encodes)
+    def _():
+        gather_x(at_once, (0, 1))
+
     @pl.when(decodes)
     def _():
-        gather_g((lambda: None, lambda: None))
-
-    links = gather(
-        xp, own_x, far_x, (s_xp, r_xp), tm_later, later, earlier, (x_hi.wait_recv, x_lo.wait_recv)
-    )
-    columns(xp, icx, False)
-    hidden()
-
-    @pl.when(decodes)
-    def _():
+        gather_g(at_once, (0, 1))
+        gather_x([link.wait_recv for link in x_links], (1, 0))
         gating()
         back_links = scatter(
-            gate, True, sent_b, got_b, sum_b, got_zb, (s_sb, r_sb), tm_earlier, earlier, later
-        )
-        for r, link in ((1, g_hi), (0, g_lo)):
-            for f in range(2):
-                back_ref[f, r] = (gp[f, r + 1].astype(jnp.float32) + inner[f, r]).astype(jnp.bfloat16)
-            link.start()
+            gate, True, sent_b, got_b, sum_b, got_zb, (s_sb, r_sb), tm_earlier, earlier, later, finish_g
+        )
         for link in back_links:
             link.wait_send()
 
-    links += scatter(
-        act, False, sent_f, got_f, sum_f, got_zf, (s_sf, r_sf), tm_later, later, earlier
+    links = scatter(
+        act, False, sent_f, got_f, sum_f, got_zf, (s_sf, r_sf), tm_later, later, earlier, finish_x
     )
-    for r, link in ((1, x_hi), (0, x_lo)):
-        for f in range(2):
-            sect_ref[f, r] = (xp[f + 2, r + 1].astype(jnp.float32) + inner[f, r]).astype(jnp.bfloat16)
-        link.start()
 
     @pl.when(encodes)
     def _():
-        gather_g((g_hi.wait_recv, g_lo.wait_recv))
+        gather_g([link.wait_recv for link in g_links], (1, 0))
         gating()
 
     def widen(n, carry):
@@ -323,7 +371,7 @@
         )
         for i in range(3):
             for j in range(3):
-                fin[pl.ds((9 * t + 3 * i + j) * 128, 128)] = product[
+                fin[pl.ds((3 * PLACES[3 * t + i] + j) * 128, 128)] = product[
                     i * 128 : (i + 1) * 128, j * 256 : (j + 1) * 256
                 ]
         product = lax.dot_general(
@@ -331,14 +379,14 @@
         )
         for i in range(3):
             for j in range(3):
-                fout[pl.ds((9 * t + 3 * i + j) * 256, 256)] = product[
+                fout[pl.ds((3 * PLACES[3 * t + i] + j) * 256, 256)] = product[
                     j * 256 : (j + 1) * 256, i * 128 : (i + 1) * 128
                 ]
 
     reduce_scatter(
         fin, fout, in_ref, out_ref, tm, core, at_y, x_at, sibling, across_y, *reduce_refs
     )
-    for link in links + [x_hi, x_lo, g_hi, g_lo]:
+    for link in links + x_links + g_links:
         link.wait_send()
 
 
@@ -359,7 +407,7 @@
         return copy
 
     def x_device(o):
-        return {"rows": at_y * 8 + x_at(o) * 2 + core}
+        return {"rows": at_y * (XS * CORES) + x_at(o) * 2 + core}
 
     def core_copy(q):
         return pltpu.make_async_remote_copy(
@@ -500,13 +548,13 @@
             vmem((4, 4, 128, 384), f32),
             vmem((2, 2) + tile, f32),
         ]
-        + [vmem((4, 2) + tile, bf16), vmem((4, 2) + tile, bf16), vmem((2, 2) + tile, bf16), vmem((2, 2) + tile, bf16)] * 2
+        + [vmem((2, 4) + tile, bf16), vmem((2, 4) + tile, bf16), vmem((2, 2) + tile, bf16), vmem((2, 2) + tile, bf16)] * 2
         + [
             vmem((512, 768), bf16),
             vmem((512, 768), bf16),
             vmem((3456, 256), f32),
             vmem((6912, 128), f32),
-            dma((6,)), dma((6,)), dma((6,)), dma((6,)), dma((5,)), dma((5,)), dma((5,)), dma((5,)), dma((4,)), dma((4,)),
+            dma((6,)), dma((6,)), dma((6,)), dma((6,)), dma((6,)), dma((6,)), dma((6,)), dma((6,)), dma((4,)), dma((4,)),
             vmem((ZS, YS, XS, CORES, CHUNK, 128), bf16),
             vmem((ZS, YS, XS, CHUNK, 128), bf16),
             vmem((2, XS, 4, YS, TOP, 128), bf16),
@@ -530,12 +578,35 @@
     )(clip, cotangent, kernel_in, kernel_out)
 
 
+def hand_over_kernel(sect_ref, in_ref, out_ref, sect_out, in_out, out_out):
+    sect_out[...] = sect_ref[...]
+    for k in range(27):
+        in_out[:, pl.ds(256 * k, 256)] = in_ref[pl.ds(k, 1)]
+    for k in range(54):
+        out_out[:, pl.ds(128 * k, 128)] = out_ref[pl.ds(k, 1)]
+
+
+def hand_over(sections, in_sum, out_sum):
+    whole = pl.BlockSpec(memory_space=pltpu.VMEM)
+    return pl.pallas_call(
+        hand_over_kernel,
+        out_shape=(
+            jax.ShapeDtypeStruct(sections.shape, sections.dtype),
+            jax.ShapeDtypeStruct((1, 6912), jnp.float32),
+            jax.ShapeDtypeStruct((1, 6912), jnp.float32),
+        ),
+        in_specs=[whole] * 3,
+        out_specs=(whole,) * 3,
+    )(sections, in_sum, out_sum)
+
+
 def on_device(tms, rows_count, input_clip, cotangent, kernel_in, kernel_out):
     sections, in_sum, out_sum = front(
         tms, rows_count, input_clip, cotangent,
         kernel_in.reshape(9, 3, 128, 256), kernel_out.reshape(9, 3, 256, 128),
     )
-    return (sections[None], in_sum.reshape(1, -1), out_sum.reshape(1, -1))
+    sections, in_sum, out_sum = hand_over(sections, in_sum, out_sum)
+    return (sections[None], in_sum, out_sum)
 
 
 def solution(mesh):

time: 102 us -> 93.2 us (0.914)
  local copies, waits for them, and re-layouts: 4.35 us -> 0 us
  Pallas kernels: 95.9 us -> 91.7 us
    pallas_call x1, Pallas kernels: 95.9 us -> 90.1 us  [front(): pl.pallas_call(partial(front_kernel, tms, rows_count), out_shape=(jax.Sha...]
    unnamed x3 -> x0, local copies, waits for them, and re-layouts: 4.35 us -> none
    pallas_call x0 -> x1, Pallas kernels: none -> 1.62 us  [hand_over(): pl.pallas_call(hand_over_kernel, out_shape=(jax.ShapeDtypeStruct(sections...]
where the time goes in v2:
time: 93.2 us; the launch traced here: 92.3 us
  Pallas kernels  91.7 us (98%)
    pallas_call x1, Pallas kernels, front(): pl.pallas_call(partial(front_kernel, tms, rows_count), out_shape=(jax.Sha...  90.1 us

profile of v2, /device:TPU:2, one launch (start us, length us, event | category | flops | bytes accessed | tf_op | source)
XLA Modules:
  0.0 92.3 jit_solution(15388654360196607191)
XLA Ops:
  0.6 90.1 %shard_map.67 = (bf16[2,2,128,128]{3,2,1,0:T(8,128)(2,1)}, f32[27,256]{1,0:T(8,128)}, f32[54,128]{1,0:T(8,128)}) custom-call(bf16[2,2,128,128]{3,2,1,0:T(8,128)(2,1)} %x_ref.1, bf16[2,2,128,128]{3,2,1,0:T(8,128)(2,1)} %g_ref.1, bf16[9,3,128,256]{3,2,1,0:T(8,128)(2,1)} %bitcast.3, bf16[9,3,256,128]{3,2,1,0:T(8,128)(2,1)} %bitcast.4), custom_call_target="tpu_custom_call" | custom-call | tf_op jit(solution)/shard_map/pallas_call | solution.py:525
  90.7 1.6 %shard_map.68 = (bf16[2,2,128,128]{3,2,1,0:T(8,128)(2,1)}, f32[1,6912]{1,0:T(1,128)}, f32[1,6912]{1,0:T(1,128)}) custom-call(bf16[2,2,128,128]{3,2,1,0:T(8,128)(2,1)} %get-tuple-element.9.sect_ref, f32[27,256]{1,0:T(8,128)} %get-tuple-element.10.in_ref, f32[54,128]{1,0:T(8,128)} %get-tuple-element.11.out_ref), custom_call_target="tpu_custom_call" | custom-call | tf_op jit(solution)/shard_map/pallas_call | solution.py:591

commit v3 on v2

--- a/solution.py
+++ b/solution.py
@@ -63,7 +63,7 @@
     tms, rows_count, x_ref, g_ref, kin_hbm, kout_hbm, sect_ref, in_ref, out_ref,
     kin_ref, kout_ref, s_load, back_ref, xp, gp, icx, icg, acc, hid, dgrad, act, gate, window, inner,
     sent_f, got_f, sum_f, got_zf, sent_b, got_b, sum_b, got_zb,
-    wide_e, wide_a, fin, fout,
+    wide_e, wide_a, act_t, icx_t, fin, fout,
     s_xp, r_xp, s_gp, r_gp, s_sf, r_sf, s_sb, r_sb, s_seg, r_seg,
     *reduce_refs,
 ):
@@ -76,6 +76,7 @@
     tm_later = {"tm": lax.rem(tm + 1, tms)}
     tm_earlier = {"tm": lax.rem(tm + tms - 1, tms)}
     other = {"segment": 1 - seg}
+    other_next = {"segment": 1 - seg, "tm": lax.rem(tm + tms + 1 - 2 * seg, tms)}
     both = jnp.logical_and
     core, at_x, at_y = lax.rem(row, 2), lax.rem(row // 2, XS), row // (XS * CORES)
 
@@ -111,7 +112,7 @@
         gp[0:2, 1:3] = g_ref[...]
 
     barrier = pltpu.get_barrier_semaphore()
-    partners = [across, other, sibling, across_y] + across_x + in_time
+    partners = [across, other, other_next, sibling, across_y] + across_x + in_time
     for partner in partners:
         pl.semaphore_signal(barrier, inc=1, device_id=partner, device_id_type=MESH_ID)
     pl.semaphore_wait(barrier, len(partners))
@@ -122,7 +123,7 @@
     outer_rows = (3 * core, 3 * (1 - core))
     row_exists = (crosses, True)
 
-    def gather(buf, own, far, sems, to, sends, receives, arrivals, order, early):
+    def gather(buf, own, far, sems, to, sends, receives, arrivals, order, early, direct=None):
         edges, times, fars = [], [], []
         for k in range(2):
             device, slot = row_devices[k], edge_slots[k]
@@ -137,18 +138,24 @@
                 Link(buf.at[far, inner_rows[k]], buf.at[far, slot], sems, 4 + k, device, crossing, crossing)
             )
         for k in order:
-            arrivals[k]()
-            times[k].start()
-            edges[k].start()
-        for k in order:
-            times[k].wait_recv()
-            fars[k].start()
+            if direct:
+                arrivals[k]()
+                edges[k].start()
+                direct[k].wait_recv()
+                fars[k].start()
+            else:
+                times[k].start()
+                edges[k].start()
+        if not direct:
+            for k in order:
+                times[k].wait_recv()
+                fars[k].start()
         for link in edges:
             link.wait_recv()
         early()
         for link in fars:
             link.wait_recv()
-        return edges + times + fars
+        return edges + fars + ([] if direct else times)
 
     def columns(buf, dest, reverse, taps):
         for n in taps:
@@ -283,7 +290,7 @@
     own_x, far_x = pl.ds(2, 2), pl.ds(0, 2)
     own_g, far_g = pl.ds(0, 2), pl.ds(2, 2)
     seg_sems = (s_seg, r_seg)
-    x_links, g_links = [], []
+    x_links, g_links, x_next, g_next = [], [], [], []
     for k in range(2):
         place = inner_rows[k]
         x_links.append(
@@ -292,21 +299,36 @@
         g_links.append(
             Link(back_ref.at[:, place - 1], gp.at[own_g, place], seg_sems, 2 + k, other, decodes, encodes)
         )
-
-    def gather_g(arrivals, order):
+        x_next.append(
+            Link(
+                sect_ref.at[:, place - 1], xp.at[far_x, place], seg_sems, 4 + k, other_next,
+                both(encodes, later), both(decodes, earlier),
+            )
+        )
+        g_next.append(
+            Link(
+                back_ref.at[:, place - 1], gp.at[far_g, place], seg_sems, 6 + k, other_next,
+                both(decodes, earlier), both(encodes, later),
+            )
+        )
+
+    def gather_g(arrivals, order, meanwhile, direct=None):
+        def early():
+            upstream_part(EARLY, False)
+            meanwhile()
+
         links = gather(
-            gp, own_g, far_g, (s_gp, r_gp), tm_earlier, earlier, later, arrivals, order,
-            lambda: upstream_part(EARLY, False),
+            gp, own_g, far_g, (s_gp, r_gp), tm_earlier, earlier, later, arrivals, order, early, direct
         )
         upstream_part(LATE, True)
         keep_upstream()
         for link in links:
             link.wait_send()
 
-    def gather_x(arrivals, order):
+    def gather_x(arrivals, order, direct=None):
         links = gather(
             xp, own_x, far_x, (s_xp, r_xp), tm_later, later, earlier, arrivals, order,
-            lambda: hidden_part(EARLY, False),
+            lambda: hidden_part(EARLY, False), direct,
         )
         hidden_part(LATE, True)
         activate()
@@ -317,14 +339,58 @@
         place = inner_rows[k]
         for f in range(2):
             sect_ref[f, place - 1] = (xp[f + 2, place].astype(jnp.float32) + sums[f]).astype(jnp.bfloat16)
+        x_next[k].start()
         x_links[k].start()
 
     def finish_g(k, sums):
         place = inner_rows[k]
         for f in range(2):
             back_ref[f, place - 1] = (gp[f, place].astype(jnp.float32) + sums[f]).astype(jnp.bfloat16)
+        g_next[k].start()
         g_links[k].start()
 
+    def widen(source, dest, by):
+        def line(n, carry):
+            at = pl.ds(pl.multiple_of(n * 128, 128), 128)
+            value = source[at].astype(jnp.float32)
+            dest[at, 0:256] = shifted(value, by).astype(jnp.bfloat16)
+            dest[at, 256:512] = source[at]
+            dest[at, 512:768] = shifted(value, -by).astype(jnp.bfloat16)
+            return carry
+
+        lax.fori_loop(0, 4, line, 0)
+
+    def prepare():
+        widen(act, wide_a, 1)
+        for n in range(6):
+            act_t[pl.ds(n * 128, 128)] = wide_a[:, pl.ds(n * 128, 128)].T
+        for n in range(9):
+            icx_t[pl.ds(n * 128, 128)] = icx[:, pl.ds(n * 128, 128)].T
+
+    def out_grad(taps):
+        span = pl.ds(PLACES.index(taps[0]) * 128, len(taps) * 128)
+        product = jnp.dot(act_t[...], icg[:, span], preferred_element_type=jnp.float32)
+        for at, n in enumerate(taps):
+            for j in range(3):
+                fout[pl.ds((3 * n + j) * 256, 256)] = product[
+                    j * 256 : (j + 1) * 256, at * 128 : (at + 1) * 128
+                ]
+
+    def in_grad():
+        widen(gate, wide_e, -1)
+        for group in range(3):
+            product = jnp.dot(
+                icx_t[pl.ds(group * 384, 384)], wide_e[...], preferred_element_type=jnp.float32
+            )
+            for i in range(3):
+                for j in range(3):
+                    fin[pl.ds((3 * PLACES[3 * group + i] + j) * 128, 128)] = product[
+                        i * 128 : (i + 1) * 128, j * 256 : (j + 1) * 256
+                    ]
+
+    begin_reduce, end_reduce = reduce_scatter(
+        fin, fout, in_ref, out_ref, tm, core, at_y, x_at, sibling, across_y, *reduce_refs
+    )
     at_once = (lambda: None, lambda: None)
     load_in.wait()
     load_out.wait()
@@ -335,14 +401,19 @@
 
     @pl.when(decodes)
     def _():
-        gather_g(at_once, (0, 1))
-        gather_x([link.wait_recv for link in x_links], (1, 0))
+        gather_g(at_once, (0, 1), lambda: None)
+        gather_x([link.wait_recv for link in x_links], (1, 0), x_next)
         gating()
         back_links = scatter(
             gate, True, sent_b, got_b, sum_b, got_zb, (s_sb, r_sb), tm_earlier, earlier, later, finish_g
         )
         for link in back_links:
             link.wait_send()
+        prepare()
+        out_grad(EARLY)
+        out_grad(LATE)
+        in_grad()
+        begin_reduce()
 
     links = scatter(
         act, False, sent_f, got_f, sum_f, got_zf, (s_sf, r_sf), tm_later, later, earlier, finish_x
@@ -350,43 +421,17 @@
 
     @pl.when(encodes)
     def _():
-        gather_g([link.wait_recv for link in g_links], (1, 0))
+        prepare()
+        gather_g(
+            [link.wait_recv for link in g_links], (1, 0), lambda: out_grad(EARLY), g_next
+        )
         gating()
-
-    def widen(n, carry):
-        at = pl.ds(pl.multiple_of(n * 128, 128), 128)
-        for source, dest, by in ((gate, wide_e, -1), (act, wide_a, 1)):
-            line = source[at].astype(jnp.float32)
-            dest[at, 0:256] = shifted(line, by).astype(jnp.bfloat16)
-            dest[at, 256:512] = source[at]
-            dest[at, 512:768] = shifted(line, -by).astype(jnp.bfloat16)
-        return carry
-
-    lax.fori_loop(0, 4, widen, 0)
-    over_cells = (((0,), (0,)), ((), ()))
-    for t in range(3):
-        span = pl.ds(t * 384, 384)
-        product = lax.dot_general(
-            icx[:, span], wide_e[...], over_cells, preferred_element_type=jnp.float32
-        )
-        for i in range(3):
-            for j in range(3):
-                fin[pl.ds((3 * PLACES[3 * t + i] + j) * 128, 128)] = product[
-                    i * 128 : (i + 1) * 128, j * 256 : (j + 1) * 256
-                ]
-        product = lax.dot_general(
-            wide_a[...], icg[:, span], over_cells, preferred_element_type=jnp.float32
-        )
-        for i in range(3):
-            for j in range(3):
-                fout[pl.ds((3 * PLACES[3 * t + i] + j) * 256, 256)] = product[
-                    j * 256 : (j + 1) * 256, i * 128 : (i + 1) * 128
-                ]
-
-    reduce_scatter(
-        fin, fout, in_ref, out_ref, tm, core, at_y, x_at, sibling, across_y, *reduce_refs
-    )
-    for link in links + x_links + g_links:
+        out_grad(LATE)
+        in_grad()
+        begin_reduce()
+
+    end_reduce()
+    for link in links + x_links + g_links + x_next + g_next:
         link.wait_send()
 
 
@@ -398,13 +443,11 @@
 ):
     f32, bf16 = jnp.float32, jnp.bfloat16
 
-    def send(src, dst, send_sem, recv_sem, device):
-        copy = pltpu.make_async_remote_copy(
+    def made(src, dst, send_sem, recv_sem, device):
+        return pltpu.make_async_remote_copy(
             src_ref=src, dst_ref=dst, send_sem=send_sem, recv_sem=recv_sem,
             device_id=device, device_id_type=MESH_ID,
         )
-        copy.start()
-        return copy
 
     def x_device(o):
         return {"rows": at_y * (XS * CORES) + x_at(o) * 2 + core}
@@ -430,90 +473,104 @@
         core_copy(q).start()
         return carry
 
-    lax.fori_loop(0, ZS, pack, 0)
-    copies = []
-    firsts = []
-    for h in range(2):
-
-        def add_core(n, carry, h=h):
-            q = 4 * h + n
-            core_copy(q).wait_recv()
-            for o in range(XS):
+    def first_copies(h):
+        copies = [
+            made(half_a.at[h, o], got_a.at[h, o], s_a.at[h, o], r_a.at[h, o], x_device(o)) for o in (2, 1, 3)
+        ]
+        return copies + [made(half_c.at[h, 1], got_c.at[h], s_c.at[h], r_c.at[h], across_y)]
+
+    def second_copies(h):
+        copies = [made(next_a.at[h], got_a2.at[h], s_a2.at[h], r_a2.at[h], across_y)]
+        return copies + [
+            made(next_c.at[h, o], got_c2.at[h, o], s_c2.at[h, o], r_c2.at[h, o], x_device(o))
+            for o in (2, 1, 3)
+        ]
+
+    def third_copy(q):
+        offset = 4 + q // 2 if q % 2 == 0 else 4 - (q + 1) // 2
+        device = {"tm": lax.rem(tm + offset, ZS)}
+        return made(last.at[q], got_z.at[q], s_z.at[q], r_z.at[q], device)
+
+    def add_core(q, carry):
+        h, n = q // 4, lax.rem(q, 4)
+        core_copy(q).wait_recv()
+        for o in range(XS):
+            for y in range(YS):
+                x = x_at(o)
+                side = lax.rem(at_y + y, 2)
+                total = blocks[q, side, x, core].astype(f32) + got_core[q, side, x].astype(f32)
+                half_a[h, o, n, y] = total[0:TOP].astype(bf16)
+                half_c[h, y, n, o] = total[TOP:CHUNK].astype(bf16)
+        return carry
+
+    def begin():
+        lax.fori_loop(0, 6, pack, 0)
+        lax.fori_loop(0, 4, add_core, 0)
+        for copy in first_copies(0):
+            copy.start()
+        lax.fori_loop(6, ZS, pack, 0)
+        lax.fori_loop(4, ZS, add_core, 0)
+        for copy in first_copies(1):
+            copy.start()
+
+    def end():
+        for h in range(2):
+            for copy in first_copies(h):
+                copy.wait_recv()
+
+            def add_first(n, carry, h=h):
                 for y in range(YS):
-                    x = x_at(o)
-                    side = lax.rem(at_y + y, 2)
-                    total = blocks[q, side, x, core].astype(f32) + got_core[q, side, x].astype(f32)
-                    half_a[h, o, n, y] = total[0:TOP].astype(bf16)
-                    half_c[h, y, n, o] = total[TOP:CHUNK].astype(bf16)
+                    total = half_a[h, 0, n, y].astype(f32)
+                    for o in range(1, XS):
+                        total = total + got_a[h, o, n, y].astype(f32)
+                    if y == 0:
+                        own_a[h, n] = total
+                    else:
+                        next_a[h, n] = total.astype(bf16)
+                for o in range(XS):
+                    total = half_c[h, 0, n, o].astype(f32) + got_c[h, n, o].astype(f32)
+                    if o == 0:
+                        own_c[h, n] = total
+                    else:
+                        next_c[h, o, n] = total.astype(bf16)
+                return carry
+
+            lax.fori_loop(0, 4, add_first, 0)
+            for copy in second_copies(h):
+                copy.start()
+        total = None
+        for h in range(2):
+            for copy in second_copies(h):
+                copy.wait_recv()
+            for n in range(4):
+                q = 4 * h + n
+                top = own_a[h, n] + got_a2[h, n].astype(f32)
+                low = own_c[h, n]
+                for o in range(1, XS):
+                    low = low + got_c2[h, o, n].astype(f32)
+                total = jnp.concatenate([top, low], axis=0)
+                if q < ZS - 1:
+                    last[q] = total.astype(bf16)
+                    third_copy(q).start()
+        for q in range(ZS - 1):
+            third_copy(q).wait_recv()
+            total = total + got_z[q].astype(f32)
+        in_ref[:, 0:128] = total[0:27]
+        in_ref[:, 128:256] = total[27:54]
+        out_ref[...] = total[54:108]
+        for h in range(2):
+            for copy in first_copies(h) + second_copies(h):
+                copy.wait_send()
+        for q in range(ZS - 1):
+            third_copy(q).wait_send()
+
+        def drain(q, carry):
+            core_copy(q).wait_send()
             return carry
 
-        lax.fori_loop(0, 4, add_core, 0)
-        sent = []
-        for o in (2, 1, 3):
-            sent.append(send(half_a.at[h, o], got_a.at[h, o], s_a.at[h, o], r_a.at[h, o], x_device(o)))
-        sent.append(send(half_c.at[h, 1], got_c.at[h], s_c.at[h], r_c.at[h], across_y))
-        firsts.append(sent)
-        copies += sent
-    seconds = []
-    for h in range(2):
-        for copy in firsts[h]:
-            copy.wait_recv()
-
-        def add_first(n, carry, h=h):
-            for y in range(YS):
-                total = half_a[h, 0, n, y].astype(f32)
-                for o in range(1, XS):
-                    total = total + got_a[h, o, n, y].astype(f32)
-                if y == 0:
-                    own_a[h, n] = total
-                else:
-                    next_a[h, n] = total.astype(bf16)
-            for o in range(XS):
-                total = half_c[h, 0, n, o].astype(f32) + got_c[h, n, o].astype(f32)
-                if o == 0:
-                    own_c[h, n] = total
-                else:
-                    next_c[h, o, n] = total.astype(bf16)
-            return carry
-
-        lax.fori_loop(0, 4, add_first, 0)
-        sent = [send(next_a.at[h], got_a2.at[h], s_a2.at[h], r_a2.at[h], across_y)]
-        for o in (2, 1, 3):
-            sent.append(send(next_c.at[h, o], got_c2.at[h, o], s_c2.at[h, o], r_c2.at[h, o], x_device(o)))
-        seconds.append(sent)
-        copies += sent
-    thirds = []
-    total = None
-    for h in range(2):
-        for copy in seconds[h]:
-            copy.wait_recv()
-        for n in range(4):
-            q = 4 * h + n
-            top = own_a[h, n] + got_a2[h, n].astype(f32)
-            low = own_c[h, n]
-            for o in range(1, XS):
-                low = low + got_c2[h, o, n].astype(f32)
-            total = jnp.concatenate([top, low], axis=0)
-            if q < ZS - 1:
-                offset = 4 + q // 2 if q % 2 == 0 else 4 - (q + 1) // 2
-                last[q] = total.astype(bf16)
-                thirds.append(
-                    send(last.at[q], got_z.at[q], s_z.at[q], r_z.at[q], {"tm": lax.rem(tm + offset, ZS)})
-                )
-    for q, copy in enumerate(thirds):
-        copy.wait_recv()
-        total = total + got_z[q].astype(f32)
-    in_ref[:, 0:128] = total[0:27]
-    in_ref[:, 128:256] = total[27:54]
-    out_ref[...] = total[54:108]
-    for copy in copies + thirds:
-        copy.wait_send()
-
-    def drain(q, carry):
-        core_copy(q).wait_send()
-        return carry
-
-    lax.fori_loop(0, ZS, drain, 0)
+        lax.fori_loop(0, ZS, drain, 0)
+
+    return begin, end
 
 
 def front(tms, rows_count, clip, cotangent, kernel_in, kernel_out):
@@ -552,9 +609,11 @@
         + [
             vmem((512, 768), bf16),
             vmem((512, 768), bf16),
+            vmem((768, 512), bf16),
+            vmem((1152, 512), bf16),
             vmem((3456, 256), f32),
             vmem((6912, 128), f32),
-            dma((6,)), dma((6,)), dma((6,)), dma((6,)), dma((6,)), dma((6,)), dma((6,)), dma((6,)), dma((4,)), dma((4,)),
+            dma((6,)), dma((6,)), dma((6,)), dma((6,)), dma((6,)), dma((6,)), dma((6,)), dma((6,)), dma((8,)), dma((8,)),
             vmem((ZS, YS, XS, CORES, CHUNK, 128), bf16),
             vmem((ZS, YS, XS, CHUNK, 128), bf16),
             vmem((2, XS, 4, YS, TOP, 128), bf16),

time: 93.2 us -> 91 us (0.976)
  Pallas kernels: 91.7 us -> 89.8 us
    pallas_call x1, Pallas kernels: 90.1 us -> 88.2 us  [front(): pl.pallas_call(partial(front_kernel, tms, rows_count), out_shape=(jax.Sha...]
where the time goes in v3:
time: 91 us; the launch traced here: 90.4 us
  Pallas kernels  89.8 us (99%)
    pallas_call x1, Pallas kernels, front(): pl.pallas_call(partial(front_kernel, tms, rows_count), out_shape=(jax.Sha...  88.2 us

profile of v3, /device:TPU:2, one launch (start us, length us, event | category | flops | bytes accessed | tf_op | source)
XLA Modules:
  0.0 90.4 jit_solution(3082879129754953952)
XLA Ops:
  0.6 88.2 %shard_map.67 = (bf16[2,2,128,128]{3,2,1,0:T(8,128)(2,1)}, f32[27,256]{1,0:T(8,128)}, f32[54,128]{1,0:T(8,128)}) custom-call(bf16[2,2,128,128]{3,2,1,0:T(8,128)(2,1)} %x_ref.1, bf16[2,2,128,128]{3,2,1,0:T(8,128)(2,1)} %g_ref.1, bf16[9,3,128,256]{3,2,1,0:T(8,128)(2,1)} %bitcast.3, bf16[9,3,256,128]{3,2,1,0:T(8,128)(2,1)} %bitcast.4), custom_call_target="tpu_custom_call" | custom-call | tf_op jit(solution)/shard_map/pallas_call | solution.py:582
  88.8 1.6 %shard_map.68 = (bf16[2,2,128,128]{3,2,1,0:T(8,128)(2,1)}, f32[1,6912]{1,0:T(1,128)}, f32[1,6912]{1,0:T(1,128)}) custom-call(bf16[2,2,128,128]{3,2,1,0:T(8,128)(2,1)} %get-tuple-element.9.sect_ref, f32[27,256]{1,0:T(8,128)} %get-tuple-element.10.in_ref, f32[54,128]{1,0:T(8,128)} %get-tuple-element.11.out_ref), custom_call_target="tpu_custom_call" | custom-call | tf_op jit(solution)/shard_map/pallas_call | solution.py:650

commit v4 on v3

--- a/solution.py
+++ b/solution.py
@@ -12,7 +12,9 @@
 CHUNK = 112
 
 
-TOP = 64
+TOP = 48
+PIECES = 4
+EACH = ZS // PIECES
 EARLY, LATE = (6, 7, 8, 1, 4), (0, 2, 3, 5)
 PLACES = EARLY + LATE
 
@@ -60,7 +62,7 @@
 
 
 def front_kernel(
-    tms, rows_count, x_ref, g_ref, kin_hbm, kout_hbm, sect_ref, in_ref, out_ref,
+    tms, rows_count, x_hbm, g_hbm, kin_hbm, kout_hbm, sect_ref, in_ref, out_ref,
     kin_ref, kout_ref, s_load, back_ref, xp, gp, icx, icg, acc, hid, dgrad, act, gate, window, inner,
     sent_f, got_f, sum_f, got_zf, sent_b, got_b, sum_b, got_zb,
     wide_e, wide_a, act_t, icx_t, fin, fout,
@@ -103,18 +105,31 @@
     got_b[...] = jnp.zeros_like(got_b)
     got_zb[...] = jnp.zeros_like(got_zb)
 
+    load_x = pltpu.make_async_copy(x_hbm, xp.at[2:4, 1:3], s_load.at[2])
+    load_g = pltpu.make_async_copy(g_hbm, gp.at[0:2, 1:3], s_load.at[3])
+
     @pl.when(encodes)
     def _():
-        xp[2:4, 1:3] = x_ref[...]
+        load_x.start()
 
     @pl.when(decodes)
     def _():
-        gp[0:2, 1:3] = g_ref[...]
+        load_g.start()
 
     barrier = pltpu.get_barrier_semaphore()
     partners = [across, other, other_next, sibling, across_y] + across_x + in_time
     for partner in partners:
         pl.semaphore_signal(barrier, inc=1, device_id=partner, device_id_type=MESH_ID)
+    window[...] = jnp.zeros_like(window)
+
+    @pl.when(encodes)
+    def _():
+        load_x.wait()
+
+    @pl.when(decodes)
+    def _():
+        load_g.wait()
+
     pl.semaphore_wait(barrier, len(partners))
 
     inner_rows = (1 + core, 2 - core)
@@ -215,54 +230,48 @@
         lax.fori_loop(0, 4, line, 0)
 
     def scatter(source, reverse, sent, got, total, got_time, sems, to, sends, receives, finish):
-        seen = set()
         own, far = (2, 0) if reverse else (0, 2)
-
-        def products(t):
-            for i in range(3):
-                n = 3 * t + i
-                if reverse:
-                    product = lax.dot_general(
-                        source[...], kin_ref[n].reshape(384, 256), (((1,), (1,)), ((), ())),
-                        preferred_element_type=jnp.float32,
-                    )
-                    a, b = t, i
-                else:
-                    weights = jnp.concatenate([kout_ref[n, j] for j in range(3)], axis=1)
-                    product = jnp.dot(source[...], weights, preferred_element_type=jnp.float32)
-                    a, b = 2 - t, 2 - i
-                for f in range(2):
-                    for r in range(2):
-                        piece = product[(2 * f + r) * 128 : (2 * f + r + 1) * 128]
-                        where = (a + f, b + r)
-                        if where in seen:
-                            window[where] += piece
-                        else:
-                            window[where] = piece
-                        seen.add(where)
+        first = 2 * core if reverse else 2 - 2 * core
+
+        def products(t, i):
+            n = 3 * t + i
+            if reverse:
+                product = lax.dot_general(
+                    source[...], kin_ref[n].reshape(384, 256), (((1,), (1,)), ((), ())),
+                    preferred_element_type=jnp.float32,
+                )
+                a, b = t, i
+            else:
+                weights = jnp.concatenate([kout_ref[n, j] for j in range(3)], axis=1)
+                product = jnp.dot(source[...], weights, preferred_element_type=jnp.float32)
+                a, b = 2 - t, 2 - i
+            for f in range(2):
+                for r in range(2):
+                    window[a + f, b + r] += product[(2 * f + r) * 128 : (2 * f + r + 1) * 128]
 
         def value(f, r):
             return joined(
                 window[f, r, :, 0:128], window[f, r, :, 128:256], window[f, r, :, 256:384], reverse
             )
 
-        def send_edges(start, base, exists):
-            links = []
-            for k in range(2):
-                for f in range(2):
-                    sent[k, start + f] = value(start + f, outer_rows[k]).astype(jnp.bfloat16)
-                span = pl.ds(start, 2)
-                goes = both(row_exists[k], exists)
-                link = Link(sent.at[k, span], got.at[k, span], sems, base + k, row_devices[k], goes, goes)
-                link.start()
-                links.append(link)
-            return links
-
-        products(0)
-        products(1)
-        far_links = send_edges(far, 0, sends)
-        products(2)
-        own_links = send_edges(own, 2, True)
+        def send_edge(k, start, index, exists):
+            for f in range(2):
+                sent[k, start + f] = value(start + f, outer_rows[k]).astype(jnp.bfloat16)
+            span = pl.ds(start, 2)
+            goes = both(row_exists[k], exists)
+            link = Link(sent.at[k, span], got.at[k, span], sems, index + k, row_devices[k], goes, goes)
+            link.start()
+            return link
+
+        far_links, own_links = [], []
+        for k, i in ((0, first), (1, 2 - first)):
+            products(0, i)
+            products(1, i)
+            far_links.append(send_edge(k, far, 0, sends))
+            products(2, i)
+            own_links.append(send_edge(k, own, 2, True))
+        for t in range(3):
+            products(t, 1)
         time_links = []
         for k in (1, 0):
             far_links[k].wait_recv()
@@ -312,8 +321,9 @@
             )
         )
 
-    def gather_g(arrivals, order, meanwhile, direct=None):
+    def gather_g(arrivals, order, ready, meanwhile, direct=None):
         def early():
+            ready()
             upstream_part(EARLY, False)
             meanwhile()
 
@@ -325,10 +335,14 @@
         for link in links:
             link.wait_send()
 
-    def gather_x(arrivals, order, direct=None):
+    def gather_x(arrivals, order, ready, direct=None):
+        def early():
+            ready()
+            hidden_part(EARLY, False)
+
         links = gather(
             xp, own_x, far_x, (s_xp, r_xp), tm_later, later, earlier, arrivals, order,
-            lambda: hidden_part(EARLY, False), direct,
+            early, direct,
         )
         hidden_part(LATE, True)
         activate()
@@ -392,21 +406,24 @@
         fin, fout, in_ref, out_ref, tm, core, at_y, x_at, sibling, across_y, *reduce_refs
     )
     at_once = (lambda: None, lambda: None)
-    load_in.wait()
-    load_out.wait()
+
+    def weights_there():
+        load_in.wait()
+        load_out.wait()
 
     @pl.when(encodes)
     def _():
-        gather_x(at_once, (0, 1))
+        gather_x(at_once, (0, 1), weights_there)
 
     @pl.when(decodes)
     def _():
-        gather_g(at_once, (0, 1), lambda: None)
-        gather_x([link.wait_recv for link in x_links], (1, 0), x_next)
+        gather_g(at_once, (0, 1), weights_there, lambda: None)
+        gather_x([link.wait_recv for link in x_links], (1, 0), lambda: None, x_next)
         gating()
         back_links = scatter(
             gate, True, sent_b, got_b, sum_b, got_zb, (s_sb, r_sb), tm_earlier, earlier, later, finish_g
         )
+        window[...] = jnp.zeros_like(window)
         for link in back_links:
             link.wait_send()
         prepare()
@@ -423,7 +440,7 @@
     def _():
         prepare()
         gather_g(
-            [link.wait_recv for link in g_links], (1, 0), lambda: out_grad(EARLY), g_next
+            [link.wait_recv for link in g_links], (1, 0), lambda: None, lambda: out_grad(EARLY), g_next
         )
         gating()
         out_grad(LATE)
@@ -492,7 +509,7 @@
         return made(last.at[q], got_z.at[q], s_z.at[q], r_z.at[q], device)
 
     def add_core(q, carry):
-        h, n = q // 4, lax.rem(q, 4)
+        h, n = q // EACH, lax.rem(q, EACH)
         core_copy(q).wait_recv()
         for o in range(XS):
             for y in range(YS):
@@ -504,61 +521,68 @@
         return carry
 
     def begin():
-        lax.fori_loop(0, 6, pack, 0)
-        lax.fori_loop(0, 4, add_core, 0)
-        for copy in first_copies(0):
+        lax.fori_loop(0, 2 * EACH, pack, 0)
+        for h in range(PIECES):
+            lax.fori_loop(h * EACH, (h + 1) * EACH, add_core, 0)
+            for copy in first_copies(h):
+                copy.start()
+            if h + 2 < PIECES:
+                lax.fori_loop((h + 2) * EACH, (h + 3) * EACH, pack, 0)
+
+    def second(h):
+        for copy in first_copies(h):
+            copy.wait_recv()
+
+        def add_first(n, carry):
+            for y in range(YS):
+                total = half_a[h, 0, n, y].astype(f32)
+                for o in range(1, XS):
+                    total = total + got_a[h, o, n, y].astype(f32)
+                if y == 0:
+                    own_a[h, n] = total
+                else:
+                    next_a[h, n] = total.astype(bf16)
+            for o in range(XS):
+                total = half_c[h, 0, n, o].astype(f32) + got_c[h, n, o].astype(f32)
+                if o == 0:
+                    own_c[h, n] = total
+                else:
+                    next_c[h, o, n] = total.astype(bf16)
+            return carry
+
+        lax.fori_loop(0, EACH, add_first, 0)
+        for copy in second_copies(h):
             copy.start()
-        lax.fori_loop(6, ZS, pack, 0)
-        lax.fori_loop(4, ZS, add_core, 0)
-        for copy in first_copies(1):
-            copy.start()
+
+    def third(h):
+        for copy in second_copies(h):
+            copy.wait_recv()
+        total = None
+        for n in range(EACH):
+            q = EACH * h + n
+            top = own_a[h, n] + got_a2[h, n].astype(f32)
+            low = own_c[h, n]
+            for o in range(1, XS):
+                low = low + got_c2[h, o, n].astype(f32)
+            total = jnp.concatenate([top, low], axis=0)
+            if q < ZS - 1:
+                last[q] = total.astype(bf16)
+                third_copy(q).start()
+        return total
 
     def end():
-        for h in range(2):
-            for copy in first_copies(h):
-                copy.wait_recv()
-
-            def add_first(n, carry, h=h):
-                for y in range(YS):
-                    total = half_a[h, 0, n, y].astype(f32)
-                    for o in range(1, XS):
-                        total = total + got_a[h, o, n, y].astype(f32)
-                    if y == 0:
-                        own_a[h, n] = total
-                    else:
-                        next_a[h, n] = total.astype(bf16)
-                for o in range(XS):
-                    total = half_c[h, 0, n, o].astype(f32) + got_c[h, n, o].astype(f32)
-                    if o == 0:
-                        own_c[h, n] = total
-                    else:
-                        next_c[h, o, n] = total.astype(bf16)
-                return carry
-
-            lax.fori_loop(0, 4, add_first, 0)
-            for copy in second_copies(h):
-                copy.start()
-        total = None
-        for h in range(2):
-            for copy in second_copies(h):
-                copy.wait_recv()
-            for n in range(4):
-                q = 4 * h + n
-                top = own_a[h, n] + got_a2[h, n].astype(f32)
-                low = own_c[h, n]
-                for o in range(1, XS):
-                    low = low + got_c2[h, o, n].astype(f32)
-                total = jnp.concatenate([top, low], axis=0)
-                if q < ZS - 1:
-                    last[q] = total.astype(bf16)
-                    third_copy(q).start()
+        second(0)
+        for h in range(1, PIECES):
+            second(h)
+            third(h - 1)
+        total = third(PIECES - 1)
         for q in range(ZS - 1):
             third_copy(q).wait_recv()
             total = total + got_z[q].astype(f32)
         in_ref[:, 0:128] = total[0:27]
         in_ref[:, 128:256] = total[27:54]
         out_ref[...] = total[54:108]
-        for h in range(2):
+        for h in range(PIECES):
             for copy in first_copies(h) + second_copies(h):
                 copy.wait_send()
         for q in range(ZS - 1):
@@ -586,12 +610,12 @@
             jax.ShapeDtypeStruct((27, 256), f32),
             jax.ShapeDtypeStruct((54, 128), f32),
         ),
-        in_specs=[whole, whole, pl.BlockSpec(memory_space=pl.ANY), pl.BlockSpec(memory_space=pl.ANY)],
+        in_specs=[pl.BlockSpec(memory_space=pl.ANY)] * 4,
         out_specs=(whole, whole, whole),
         scratch_shapes=[
             vmem((9, 3, 128, 256), bf16),
             vmem((9, 3, 256, 128), bf16),
-            dma((2,)),
+            dma((4,)),
             vmem((2, 2) + tile, bf16),
             vmem((4, 4) + tile, bf16),
             vmem((4, 4) + tile, bf16),
@@ -616,20 +640,20 @@
             dma((6,)), dma((6,)), dma((6,)), dma((6,)), dma((6,)), dma((6,)), dma((6,)), dma((6,)), dma((8,)), dma((8,)),
             vmem((ZS, YS, XS, CORES, CHUNK, 128), bf16),
             vmem((ZS, YS, XS, CHUNK, 128), bf16),
-            vmem((2, XS, 4, YS, TOP, 128), bf16),
-            vmem((2, XS, 4, YS, TOP, 128), bf16),
-            vmem((2, YS, 4, XS, CHUNK - TOP, 128), bf16),
-            vmem((2, 4, XS, CHUNK - TOP, 128), bf16),
-            vmem((2, 4, TOP, 128), bf16),
-            vmem((2, 4, TOP, 128), bf16),
-            vmem((2, XS, 4, CHUNK - TOP, 128), bf16),
-            vmem((2, XS, 4, CHUNK - TOP, 128), bf16),
-            vmem((2, 4, TOP, 128), f32),
-            vmem((2, 4, CHUNK - TOP, 128), f32),
+            vmem((PIECES, XS, EACH, YS, TOP, 128), bf16),
+            vmem((PIECES, XS, EACH, YS, TOP, 128), bf16),
+            vmem((PIECES, YS, EACH, XS, CHUNK - TOP, 128), bf16),
+            vmem((PIECES, EACH, XS, CHUNK - TOP, 128), bf16),
+            vmem((PIECES, EACH, TOP, 128), bf16),
+            vmem((PIECES, EACH, TOP, 128), bf16),
+            vmem((PIECES, XS, EACH, CHUNK - TOP, 128), bf16),
+            vmem((PIECES, XS, EACH, CHUNK - TOP, 128), bf16),
+            vmem((PIECES, EACH, TOP, 128), f32),
+            vmem((PIECES, EACH, CHUNK - TOP, 128), f32),
             vmem((ZS, CHUNK, 128), bf16),
             vmem((ZS, CHUNK, 128), bf16),
-            dma((ZS,)), dma((ZS,)), dma((2, XS)), dma((2, XS)), dma((2,)), dma((2,)),
-            dma((2,)), dma((2,)), dma((2, XS)), dma((2, XS)), dma((ZS,)), dma((ZS,)),
+            dma((ZS,)), dma((ZS,)), dma((PIECES, XS)), dma((PIECES, XS)), dma((PIECES,)), dma((PIECES,)),
+            dma((PIECES,)), dma((PIECES,)), dma((PIECES, XS)), dma((PIECES, XS)), dma((ZS,)), dma((ZS,)),
         ],
         compiler_params=pltpu.CompilerParams(
             collective_id=1, has_side_effects=True, vmem_limit_bytes=56 << 20

time: 91 us -> 88.2 us (0.969)
  the two profiles are of different devices: /device:TPU:2 before, /device:TPU:1 now
where the time goes in v4:
time: 88.2 us; the launch traced here: 88.1 us
  Pallas kernels  87.4 us (99%)
    pallas_call x1, Pallas kernels, front(): pl.pallas_call(partial(front_kernel, tms, rows_count), out_shape=(jax.Sha...  85.8 us

profile of v4, /device:TPU:1, one launch (start us, length us, event | category | flops | bytes accessed | tf_op | source)
XLA Modules:
  0.0 88.1 jit_solution(16736723860591901825)
XLA Ops:
  0.6 85.8 %shard_map.67 = (bf16[2,2,128,128]{3,2,1,0:T(8,128)(2,1)}, f32[27,256]{1,0:T(8,128)}, f32[54,128]{1,0:T(8,128)}) custom-call(bf16[2,2,128,128]{3,2,1,0:T(8,128)(2,1)} %x_hbm.1, bf16[2,2,128,128]{3,2,1,0:T(8,128)(2,1)} %g_hbm.1, bf16[9,3,128,256]{3,2,1,0:T(8,128)(2,1)} %bitcast.3, bf16[9,3,256,128]{3,2,1,0:T(8,128)(2,1)} %bitcast.4), custom_call_target="tpu_custom_call" | custom-call | tf_op jit(solution)/shard_map/pallas_call | solution.py:606
  86.4 1.6 %shard_map.68 = (bf16[2,2,128,128]{3,2,1,0:T(8,128)(2,1)}, f32[1,6912]{1,0:T(1,128)}, f32[1,6912]{1,0:T(1,128)}) custom-call(bf16[2,2,128,128]{3,2,1,0:T(8,128)(2,1)} %get-tuple-element.9.sect_ref, f32[27,256]{1,0:T(8,128)} %get-tuple-element.10.in_ref, f32[54,128]{1,0:T(8,128)} %get-tuple-element.11.out_ref), custom_call_target="tpu_custom_call" | custom-call | tf_op jit(solution)/shard_map/pallas_call | solution.py:674

commit v5 on v4

--- a/solution.py
+++ b/solution.py
@@ -12,7 +12,7 @@
 CHUNK = 112
 
 
-TOP = 48
+TOP = 56
 PIECES = 4
 EACH = ZS // PIECES
 EARLY, LATE = (6, 7, 8, 1, 4), (0, 2, 3, 5)
@@ -62,8 +62,8 @@
 
 
 def front_kernel(
-    tms, rows_count, x_hbm, g_hbm, kin_hbm, kout_hbm, sect_ref, in_ref, out_ref,
-    kin_ref, kout_ref, s_load, back_ref, xp, gp, icx, icg, acc, hid, dgrad, act, gate, window, inner,
+    tms, rows_count, x_hbm, g_hbm, kin_hbm, kout_hbm, sect_hbm, in_ref, out_ref,
+    sect_ref, kin_ref, kout_ref, s_load, back_ref, xp, gp, icx, icg, acc, slope, dgrad, act, gate, window, inner,
     sent_f, got_f, sum_f, got_zf, sent_b, got_b, sum_b, got_zb,
     wide_e, wide_a, act_t, icx_t, fin, fout,
     s_xp, r_xp, s_gp, r_gp, s_sf, r_sf, s_sb, r_sb, s_seg, r_seg,
@@ -138,7 +138,7 @@
     outer_rows = (3 * core, 3 * (1 - core))
     row_exists = (crosses, True)
 
-    def gather(buf, own, far, sems, to, sends, receives, arrivals, order, early, direct=None):
+    def gather(buf, own, far, sems, to, sends, receives, arrivals, early, direct=None):
         edges, times, fars = [], [], []
         for k in range(2):
             device, slot = row_devices[k], edge_slots[k]
@@ -152,17 +152,21 @@
             fars.append(
                 Link(buf.at[far, inner_rows[k]], buf.at[far, slot], sems, 4 + k, device, crossing, crossing)
             )
-        for k in order:
-            if direct:
-                arrivals[k]()
-                edges[k].start()
-                direct[k].wait_recv()
-                fars[k].start()
-            else:
+        if direct:
+            arrivals[1]()
+            times[1].start()
+            edges[1].start()
+            direct.wait_recv()
+            fars[0].start()
+            arrivals[0]()
+            edges[0].start()
+            times[1].wait_recv()
+            fars[1].start()
+        else:
+            for k in (0, 1):
                 times[k].start()
                 edges[k].start()
-        if not direct:
-            for k in order:
+            for k in (0, 1):
                 times[k].wait_recv()
                 fars[k].start()
         for link in edges:
@@ -170,7 +174,7 @@
         early()
         for link in fars:
             link.wait_recv()
-        return edges + fars + ([] if direct else times)
+        return edges + fars + (times[1:] if direct else times)
 
     def columns(buf, dest, reverse, taps):
         for n in taps:
@@ -205,8 +209,9 @@
         def line(n, carry):
             at = pl.ds(pl.multiple_of(n * 128, 128), 128)
             value = joined(acc[0, at], acc[1, at], acc[2, at], False)
-            hid[at] = value
-            act[at] = (value / (1.0 + jnp.exp(-value))).astype(jnp.bfloat16)
+            sigmoid = 1.0 / (1.0 + jnp.exp(-value))
+            slope[at] = sigmoid * (1.0 + value * (1.0 - sigmoid))
+            act[at] = (value * sigmoid).astype(jnp.bfloat16)
             return carry
 
         lax.fori_loop(0, 4, line, 0)
@@ -222,9 +227,7 @@
     def gating():
         def line(n, carry):
             at = pl.ds(pl.multiple_of(n * 128, 128), 128)
-            value = hid[at]
-            sigmoid = 1.0 / (1.0 + jnp.exp(-value))
-            gate[at] = (dgrad[at] * sigmoid * (1.0 + value * (1.0 - sigmoid))).astype(jnp.bfloat16)
+            gate[at] = (dgrad[at] * slope[at]).astype(jnp.bfloat16)
             return carry
 
         lax.fori_loop(0, 4, line, 0)
@@ -299,7 +302,7 @@
     own_x, far_x = pl.ds(2, 2), pl.ds(0, 2)
     own_g, far_g = pl.ds(0, 2), pl.ds(2, 2)
     seg_sems = (s_seg, r_seg)
-    x_links, g_links, x_next, g_next = [], [], [], []
+    x_links, g_links = [], []
     for k in range(2):
         place = inner_rows[k]
         x_links.append(
@@ -308,40 +311,36 @@
         g_links.append(
             Link(back_ref.at[:, place - 1], gp.at[own_g, place], seg_sems, 2 + k, other, decodes, encodes)
         )
-        x_next.append(
-            Link(
-                sect_ref.at[:, place - 1], xp.at[far_x, place], seg_sems, 4 + k, other_next,
-                both(encodes, later), both(decodes, earlier),
-            )
-        )
-        g_next.append(
-            Link(
-                back_ref.at[:, place - 1], gp.at[far_g, place], seg_sems, 6 + k, other_next,
-                both(decodes, earlier), both(encodes, later),
-            )
-        )
-
-    def gather_g(arrivals, order, ready, meanwhile, direct=None):
+    x_next = Link(
+        sect_ref.at[:, core], xp.at[far_x, 1 + core], seg_sems, 4, other_next,
+        both(encodes, later), both(decodes, earlier),
+    )
+    g_next = Link(
+        back_ref.at[:, core], gp.at[far_g, 1 + core], seg_sems, 5, other_next,
+        both(decodes, earlier), both(encodes, later),
+    )
+
+    def gather_g(arrivals, ready, meanwhile, direct=None):
         def early():
             ready()
             upstream_part(EARLY, False)
             meanwhile()
 
         links = gather(
-            gp, own_g, far_g, (s_gp, r_gp), tm_earlier, earlier, later, arrivals, order, early, direct
+            gp, own_g, far_g, (s_gp, r_gp), tm_earlier, earlier, later, arrivals, early, direct
         )
         upstream_part(LATE, True)
         keep_upstream()
         for link in links:
             link.wait_send()
 
-    def gather_x(arrivals, order, ready, direct=None):
+    def gather_x(arrivals, ready, direct=None):
         def early():
             ready()
             hidden_part(EARLY, False)
 
         links = gather(
-            xp, own_x, far_x, (s_xp, r_xp), tm_later, later, earlier, arrivals, order,
+            xp, own_x, far_x, (s_xp, r_xp), tm_later, later, earlier, arrivals,
             early, direct,
         )
         hidden_part(LATE, True)
@@ -353,14 +352,16 @@
         place = inner_rows[k]
         for f in range(2):
             sect_ref[f, place - 1] = (xp[f + 2, place].astype(jnp.float32) + sums[f]).astype(jnp.bfloat16)
-        x_next[k].start()
+        if k == 0:
+            x_next.start()
         x_links[k].start()
 
     def finish_g(k, sums):
         place = inner_rows[k]
         for f in range(2):
             back_ref[f, place - 1] = (gp[f, place].astype(jnp.float32) + sums[f]).astype(jnp.bfloat16)
-        g_next[k].start()
+        if k == 0:
+            g_next.start()
         g_links[k].start()
 
     def widen(source, dest, by):
@@ -405,7 +406,6 @@
     begin_reduce, end_reduce = reduce_scatter(
         fin, fout, in_ref, out_ref, tm, core, at_y, x_at, sibling, across_y, *reduce_refs
     )
-    at_once = (lambda: None, lambda: None)
 
     def weights_there():
         load_in.wait()
@@ -413,12 +413,12 @@
 
     @pl.when(encodes)
     def _():
-        gather_x(at_once, (0, 1), weights_there)
+        gather_x(None, weights_there)
 
     @pl.when(decodes)
     def _():
-        gather_g(at_once, (0, 1), weights_there, lambda: None)
-        gather_x([link.wait_recv for link in x_links], (1, 0), lambda: None, x_next)
+        gather_g(None, weights_there, lambda: None)
+        gather_x([link.wait_recv for link in x_links], lambda: None, x_next)
         gating()
         back_links = scatter(
             gate, True, sent_b, got_b, sum_b, got_zb, (s_sb, r_sb), tm_earlier, earlier, later, finish_g
@@ -440,15 +440,18 @@
     def _():
         prepare()
         gather_g(
-            [link.wait_recv for link in g_links], (1, 0), lambda: None, lambda: out_grad(EARLY), g_next
+            [link.wait_recv for link in g_links], lambda: None, lambda: out_grad(EARLY), g_next
         )
         gating()
         out_grad(LATE)
         in_grad()
         begin_reduce()
 
+    store = pltpu.make_async_copy(sect_ref, sect_hbm, s_load.at[4])
+    store.start()
     end_reduce()
-    for link in links + x_links + g_links + x_next + g_next:
+    store.wait()
+    for link in links + x_links + g_links + [x_next, g_next]:
         link.wait_send()
 
 
@@ -611,11 +614,12 @@
             jax.ShapeDtypeStruct((54, 128), f32),
         ),
         in_specs=[pl.BlockSpec(memory_space=pl.ANY)] * 4,
-        out_specs=(whole, whole, whole),
+        out_specs=(pl.BlockSpec(memory_space=pl.ANY), whole, whole),
         scratch_shapes=[
+            vmem((2, 2) + tile, bf16),
             vmem((9, 3, 128, 256), bf16),
             vmem((9, 3, 256, 128), bf16),
-            dma((4,)),
+            dma((5,)),
             vmem((2, 2) + tile, bf16),
             vmem((4, 4) + tile, bf16),
             vmem((4, 4) + tile, bf16),
@@ -637,7 +641,7 @@
             vmem((1152, 512), bf16),
             vmem((3456, 256), f32),
             vmem((6912, 128), f32),
-            dma((6,)), dma((6,)), dma((6,)), dma((6,)), dma((6,)), dma((6,)), dma((6,)), dma((6,)), dma((8,)), dma((8,)),
+            dma((6,)), dma((6,)), dma((6,)), dma((6,)), dma((6,)), dma((6,)), dma((6,)), dma((6,)), dma((6,)), dma((6,)),
             vmem((ZS, YS, XS, CORES, CHUNK, 128), bf16),
             vmem((ZS, YS, XS, CHUNK, 128), bf16),
             vmem((PIECES, XS, EACH, YS, TOP, 128), bf16),
@@ -661,16 +665,18 @@
     )(clip, cotangent, kernel_in, kernel_out)
 
 
-def hand_over_kernel(sect_ref, in_ref, out_ref, sect_out, in_out, out_out):
-    sect_out[...] = sect_ref[...]
+def hand_over_kernel(sect_hbm, in_ref, out_ref, sect_out, in_out, out_out, sem):
+    copy = pltpu.make_async_copy(sect_hbm, sect_out, sem)
+    copy.start()
     for k in range(27):
         in_out[:, pl.ds(256 * k, 256)] = in_ref[pl.ds(k, 1)]
     for k in range(54):
         out_out[:, pl.ds(128 * k, 128)] = out_ref[pl.ds(k, 1)]
+    copy.wait()
 
 
 def hand_over(sections, in_sum, out_sum):
-    whole = pl.BlockSpec(memory_space=pltpu.VMEM)
+    whole, anywhere = pl.BlockSpec(memory_space=pltpu.VMEM), pl.BlockSpec(memory_space=pl.ANY)
     return pl.pallas_call(
         hand_over_kernel,
         out_shape=(
@@ -678,8 +684,9 @@
             jax.ShapeDtypeStruct((1, 6912), jnp.float32),
             jax.ShapeDtypeStruct((1, 6912), jnp.float32),
         ),
-        in_specs=[whole] * 3,
-        out_specs=(whole,) * 3,
+        in_specs=[anywhere, whole, whole],
+        out_specs=(anywhere, whole, whole),
+        scratch_shapes=[pltpu.SemaphoreType.DMA],
     )(sections, in_sum, out_sum)
 
 

time: 88.2 us -> 93.8 us (1.063)
  the two profiles are of different devices: /device:TPU:1 before, /device:TPU:2 now
where the time goes in v5:
time: 93.8 us; the launch traced here: 93.1 us
  Pallas kernels  92.3 us (98%)
    pallas_call x1, Pallas kernels, front(): pl.pallas_call(partial(front_kernel, tms, rows_count), out_shape=(jax.Sha...  85.8 us
    pallas_call x1, Pallas kernels, hand_over(): pl.pallas_call(hand_over_kernel, out_shape=(jax.ShapeDtypeStruct(sections...  6.46 us

profile of v5, /device:TPU:2, one launch (start us, length us, event | category | flops | bytes accessed | tf_op | source)
XLA Modules:
  0.0 93.1 jit_solution(7638935347100598265)
XLA Ops:
  0.6 85.8 %shard_map.67 = (bf16[2,2,128,128]{3,2,1,0:T(8,128)(2,1)}, f32[27,256]{1,0:T(8,128)}, f32[54,128]{1,0:T(8,128)}) custom-call(bf16[2,2,128,128]{3,2,1,0:T(8,128)(2,1)} %x_hbm.1, bf16[2,2,128,128]{3,2,1,0:T(8,128)(2,1)} %g_hbm.1, bf16[9,3,128,256]{3,2,1,0:T(8,128)(2,1)} %bitcast.3, bf16[9,3,256,128]{3,2,1,0:T(8,128)(2,1)} %bitcast.4), custom_call_target="tpu_custom_call" | custom-call | tf_op jit(solution)/shard_map/pallas_call | solution.py:609
  86.4 6.5 %shard_map.68 = (bf16[2,2,128,128]{3,2,1,0:T(8,128)(2,1)}, f32[1,6912]{1,0:T(1,128)}, f32[1,6912]{1,0:T(1,128)}) custom-call(bf16[2,2,128,128]{3,2,1,0:T(8,128)(2,1)} %get-tuple-element.9.sect_hbm, f32[27,256]{1,0:T(8,128)} %get-tuple-element.10.in_ref, f32[54,128]{1,0:T(8,128)} %get-tuple-element.11.out_ref), custom_call_target="tpu_custom_call" | custom-call | tf_op jit(solution)/shard_map/pallas_call | solution.py:680

commit v6 on v5

--- a/solution.py
+++ b/solution.py
@@ -12,8 +12,8 @@
 CHUNK = 112
 
 
-TOP = 56
-PIECES = 4
+TOP = 48
+PIECES = 2
 EACH = ZS // PIECES
 EARLY, LATE = (6, 7, 8, 1, 4), (0, 2, 3, 5)
 PLACES = EARLY + LATE
@@ -84,7 +84,14 @@
 
     step = 2 * core - 1
     crosses = both(row + step >= 0, row + step < rows_count)
-    across = {"rows": lax.rem(row + step + rows_count, rows_count)}
+    across_row = lax.rem(row + step + rows_count, rows_count)
+    across = {"rows": across_row}
+    border = both(crosses, at_y != across_row // (XS * CORES))
+    inside = jnp.logical_not(border)
+    other_across = {"segment": 1 - seg, "rows": across_row}
+    other_across_next = {
+        "segment": 1 - seg, "tm": lax.rem(tm + tms + 1 - 2 * seg, tms), "rows": across_row
+    }
 
     def x_at(offset):
         return lax.rem(at_x + offset, XS)
@@ -117,7 +124,7 @@
         load_g.start()
 
     barrier = pltpu.get_barrier_semaphore()
-    partners = [across, other, other_next, sibling, across_y] + across_x + in_time
+    partners = [across, other, other_next, other_across, other_across_next, sibling, across_y] + across_x + in_time
     for partner in partners:
         pl.semaphore_signal(barrier, inc=1, device_id=partner, device_id_type=MESH_ID)
     window[...] = jnp.zeros_like(window)
@@ -142,13 +149,14 @@
         edges, times, fars = [], [], []
         for k in range(2):
             device, slot = row_devices[k], edge_slots[k]
+            exists = both(row_exists[k], inside) if direct and k == 0 else row_exists[k]
             edges.append(
-                Link(buf.at[own, inner_rows[k]], buf.at[own, slot], sems, k, device, row_exists[k], row_exists[k])
+                Link(buf.at[own, inner_rows[k]], buf.at[own, slot], sems, k, device, exists, exists)
             )
             times.append(
                 Link(buf.at[own, inner_rows[k]], buf.at[far, inner_rows[k]], sems, 2 + k, to, sends, receives)
             )
-            crossing = both(row_exists[k], receives)
+            crossing = both(exists, receives)
             fars.append(
                 Link(buf.at[far, inner_rows[k]], buf.at[far, slot], sems, 4 + k, device, crossing, crossing)
             )
@@ -156,7 +164,7 @@
             arrivals[1]()
             times[1].start()
             edges[1].start()
-            direct.wait_recv()
+            direct[0].wait_recv()
             fars[0].start()
             arrivals[0]()
             edges[0].start()
@@ -169,10 +177,10 @@
             for k in (0, 1):
                 times[k].wait_recv()
                 fars[k].start()
-        for link in edges:
+        for link in edges + (direct[2:] if direct else []):
             link.wait_recv()
         early()
-        for link in fars:
+        for link in fars + (direct[1:2] if direct else []):
             link.wait_recv()
         return edges + fars + (times[1:] if direct else times)
 
@@ -311,13 +319,25 @@
         g_links.append(
             Link(back_ref.at[:, place - 1], gp.at[own_g, place], seg_sems, 2 + k, other, decodes, encodes)
         )
-    x_next = Link(
-        sect_ref.at[:, core], xp.at[far_x, 1 + core], seg_sems, 4, other_next,
-        both(encodes, later), both(decodes, earlier),
+    def straight(src, buf, own, far, index, sends, receives, sends_next, receives_next):
+        row_ref, place, slot = src.at[:, core], 1 + core, edge_slots[0]
+        return [
+            Link(row_ref, buf.at[far, place], seg_sems, index, other_next, sends_next, receives_next),
+            Link(
+                row_ref, buf.at[far, slot], seg_sems, index + 1, other_across_next,
+                both(sends_next, border), both(receives_next, border),
+            ),
+            Link(
+                row_ref, buf.at[own, slot], seg_sems, index + 2, other_across,
+                both(sends, border), both(receives, border),
+            ),
+        ]
+
+    x_next = straight(
+        sect_ref, xp, own_x, far_x, 4, encodes, decodes, both(encodes, later), both(decodes, earlier)
     )
-    g_next = Link(
-        back_ref.at[:, core], gp.at[far_g, 1 + core], seg_sems, 5, other_next,
-        both(decodes, earlier), both(encodes, later),
+    g_next = straight(
+        back_ref, gp, own_g, far_g, 7, decodes, encodes, both(decodes, earlier), both(encodes, later)
     )
 
     def gather_g(arrivals, ready, meanwhile, direct=None):
@@ -353,7 +373,8 @@
         for f in range(2):
             sect_ref[f, place - 1] = (xp[f + 2, place].astype(jnp.float32) + sums[f]).astype(jnp.bfloat16)
         if k == 0:
-            x_next.start()
+            for link in x_next:
+                link.start()
         x_links[k].start()
 
     def finish_g(k, sums):
@@ -361,7 +382,8 @@
         for f in range(2):
             back_ref[f, place - 1] = (gp[f, place].astype(jnp.float32) + sums[f]).astype(jnp.bfloat16)
         if k == 0:
-            g_next.start()
+            for link in g_next:
+                link.start()
         g_links[k].start()
 
     def widen(source, dest, by):
@@ -451,7 +473,7 @@
     store.start()
     end_reduce()
     store.wait()
-    for link in links + x_links + g_links + [x_next, g_next]:
+    for link in links + x_links + g_links + x_next + g_next:
         link.wait_send()
 
 
@@ -641,7 +663,7 @@
             vmem((1152, 512), bf16),
             vmem((3456, 256), f32),
             vmem((6912, 128), f32),
-            dma((6,)), dma((6,)), dma((6,)), dma((6,)), dma((6,)), dma((6,)), dma((6,)), dma((6,)), dma((6,)), dma((6,)),
+            dma((6,)), dma((6,)), dma((6,)), dma((6,)), dma((6,)), dma((6,)), dma((6,)), dma((6,)), dma((10,)), dma((10,)),
             vmem((ZS, YS, XS, CORES, CHUNK, 128), bf16),
             vmem((ZS, YS, XS, CHUNK, 128), bf16),
             vmem((PIECES, XS, EACH, YS, TOP, 128), bf16),
@@ -665,18 +687,16 @@
     )(clip, cotangent, kernel_in, kernel_out)
 
 
-def hand_over_kernel(sect_hbm, in_ref, out_ref, sect_out, in_out, out_out, sem):
-    copy = pltpu.make_async_copy(sect_hbm, sect_out, sem)
-    copy.start()
+def hand_over_kernel(sect_ref, in_ref, out_ref, sect_out, in_out, out_out):
+    sect_out[...] = sect_ref[...]
     for k in range(27):
         in_out[:, pl.ds(256 * k, 256)] = in_ref[pl.ds(k, 1)]
     for k in range(54):
         out_out[:, pl.ds(128 * k, 128)] = out_ref[pl.ds(k, 1)]
-    copy.wait()
 
 
 def hand_over(sections, in_sum, out_sum):
-    whole, anywhere = pl.BlockSpec(memory_space=pltpu.VMEM), pl.BlockSpec(memory_space=pl.ANY)
+    whole = pl.BlockSpec(memory_space=pltpu.VMEM)
     return pl.pallas_call(
         hand_over_kernel,
         out_shape=(
@@ -684,9 +704,8 @@
             jax.ShapeDtypeStruct((1, 6912), jnp.float32),
             jax.ShapeDtypeStruct((1, 6912), jnp.float32),
         ),
-        in_specs=[anywhere, whole, whole],
-        out_specs=(anywhere, whole, whole),
-        scratch_shapes=[pltpu.SemaphoreType.DMA],
+        in_specs=[whole] * 3,
+        out_specs=(whole,) * 3,
     )(sections, in_sum, out_sum)
 
 

time: 93.8 us -> 84.1 us (0.90)
  Pallas kernels: 92.3 us -> 82.2 us
    pallas_call x1, Pallas kernels: 85.8 us -> 80.5 us  [front(): pl.pallas_call(partial(front_kernel, tms, rows_count), out_shape=(jax.Sha...]
    pallas_call x1, Pallas kernels: 6.46 us -> 1.62 us  [hand_over(): pl.pallas_call(hand_over_kernel, out_shape=(jax.ShapeDtypeStruct(sections...]
where the time goes in v6:
time: 84.1 us; the launch traced here: 82.8 us
  Pallas kernels  82.2 us (98%)
    pallas_call x1, Pallas kernels, front(): pl.pallas_call(partial(front_kernel, tms, rows_count), out_shape=(jax.Sha...  80.5 us

profile of v6, /device:TPU:2, one launch (start us, length us, event | category | flops | bytes accessed | tf_op | source)
XLA Modules:
  0.0 82.8 jit_solution(3231465098344067404)
XLA Ops:
  0.6 80.5 %shard_map.67 = (bf16[2,2,128,128]{3,2,1,0:T(8,128)(2,1)}, f32[27,256]{1,0:T(8,128)}, f32[54,128]{1,0:T(8,128)}) custom-call(bf16[2,2,128,128]{3,2,1,0:T(8,128)(2,1)} %x_hbm.1, bf16[2,2,128,128]{3,2,1,0:T(8,128)(2,1)} %g_hbm.1, bf16[9,3,128,256]{3,2,1,0:T(8,128)(2,1)} %bitcast.3, bf16[9,3,256,128]{3,2,1,0:T(8,128)(2,1)} %bitcast.4), custom_call_target="tpu_custom_call" | custom-call | tf_op jit(solution)/shard_map/pallas_call | solution.py:631
  81.2 1.6 %shard_map.68 = (bf16[2,2,128,128]{3,2,1,0:T(8,128)(2,1)}, f32[1,6912]{1,0:T(1,128)}, f32[1,6912]{1,0:T(1,128)}) custom-call(bf16[2,2,128,128]{3,2,1,0:T(8,128)(2,1)} %get-tuple-element.9.sect_ref, f32[27,256]{1,0:T(8,128)} %get-tuple-element.10.in_ref, f32[54,128]{1,0:T(8,128)} %get-tuple-element.11.out_ref), custom_call_target="tpu_custom_call" | custom-call | tf_op jit(solution)/shard_map/pallas_call | solution.py:700

commit v7 on v6

--- a/solution.py
+++ b/solution.py
@@ -12,8 +12,8 @@
 CHUNK = 112
 
 
-TOP = 48
-PIECES = 2
+TOP = 56
+PIECES = 4
 EACH = ZS // PIECES
 EARLY, LATE = (6, 7, 8, 1, 4), (0, 2, 3, 5)
 PLACES = EARLY + LATE
@@ -63,7 +63,7 @@
 
 def front_kernel(
     tms, rows_count, x_hbm, g_hbm, kin_hbm, kout_hbm, sect_hbm, in_ref, out_ref,
-    sect_ref, kin_ref, kout_ref, s_load, back_ref, xp, gp, icx, icg, acc, slope, dgrad, act, gate, window, inner,
+    sect_ref, corner_x, kin_ref, kout_ref, s_load, back_ref, xp, gp, icx, icg, acc, slope, dgrad, act, gate, window, inner,
     sent_f, got_f, sum_f, got_zf, sent_b, got_b, sum_b, got_zb,
     wide_e, wide_a, act_t, icx_t, fin, fout,
     s_xp, r_xp, s_gp, r_gp, s_sf, r_sf, s_sb, r_sb, s_seg, r_seg,
@@ -89,6 +89,9 @@
     border = both(crosses, at_y != across_row // (XS * CORES))
     inside = jnp.logical_not(border)
     other_across = {"segment": 1 - seg, "rows": across_row}
+    other_across_past = {
+        "segment": 1 - seg, "tm": lax.rem(tm + tms + 2 * seg - 1, tms), "rows": across_row
+    }
     other_across_next = {
         "segment": 1 - seg, "tm": lax.rem(tm + tms + 1 - 2 * seg, tms), "rows": across_row
     }
@@ -113,6 +116,7 @@
     got_zb[...] = jnp.zeros_like(got_zb)
 
     load_x = pltpu.make_async_copy(x_hbm, xp.at[2:4, 1:3], s_load.at[2])
+    load_corner = pltpu.make_async_copy(x_hbm, corner_x, s_load.at[2])
     load_g = pltpu.make_async_copy(g_hbm, gp.at[0:2, 1:3], s_load.at[3])
 
     @pl.when(encodes)
@@ -121,10 +125,11 @@
 
     @pl.when(decodes)
     def _():
+        load_corner.start()
         load_g.start()
 
     barrier = pltpu.get_barrier_semaphore()
-    partners = [across, other, other_next, other_across, other_across_next, sibling, across_y] + across_x + in_time
+    partners = [across, other, other_next, other_across, other_across_next, other_across_past, sibling, across_y] + across_x + in_time
     for partner in partners:
         pl.semaphore_signal(barrier, inc=1, device_id=partner, device_id_type=MESH_ID)
     window[...] = jnp.zeros_like(window)
@@ -135,6 +140,7 @@
 
     @pl.when(decodes)
     def _():
+        load_corner.wait()
         load_g.wait()
 
     pl.semaphore_wait(barrier, len(partners))
@@ -145,7 +151,7 @@
     outer_rows = (3 * core, 3 * (1 - core))
     row_exists = (crosses, True)
 
-    def gather(buf, own, far, sems, to, sends, receives, arrivals, early, direct=None):
+    def gather(buf, own, far, sems, to, sends, receives, arrivals, early, direct=None, corner=None):
         edges, times, fars = [], [], []
         for k in range(2):
             device, slot = row_devices[k], edge_slots[k]
@@ -170,6 +176,14 @@
             edges[0].start()
             times[1].wait_recv()
             fars[1].start()
+        elif corner:
+            for k in (1, 0):
+                times[k].start()
+                edges[1 - k].start()
+            times[1].wait_recv()
+            fars[1].start()
+            times[0].wait_recv()
+            fars = [corner, fars[1]]
         else:
             for k in (0, 1):
                 times[k].start()
@@ -182,7 +196,7 @@
         early()
         for link in fars + (direct[1:2] if direct else []):
             link.wait_recv()
-        return edges + fars + (times[1:] if direct else times)
+        return edges + (fars[1:] if corner else fars) + (times[1:] if direct else times)
 
     def columns(buf, dest, reverse, taps):
         for n in taps:
@@ -340,6 +354,11 @@
         back_ref, gp, own_g, far_g, 7, decodes, encodes, both(decodes, earlier), both(encodes, later)
     )
 
+    corner = Link(
+        corner_x.at[:, core], xp.at[far_x, edge_slots[0]], seg_sems, 10, other_across_past,
+        both(both(decodes, crosses), later), both(both(encodes, crosses), earlier),
+    )
+
     def gather_g(arrivals, ready, meanwhile, direct=None):
         def early():
             ready()
@@ -354,14 +373,14 @@
         for link in links:
             link.wait_send()
 
-    def gather_x(arrivals, ready, direct=None):
+    def gather_x(arrivals, ready, direct=None, corner=None):
         def early():
             ready()
             hidden_part(EARLY, False)
 
         links = gather(
             xp, own_x, far_x, (s_xp, r_xp), tm_later, later, earlier, arrivals,
-            early, direct,
+            early, direct, corner,
         )
         hidden_part(LATE, True)
         activate()
@@ -435,10 +454,11 @@
 
     @pl.when(encodes)
     def _():
-        gather_x(None, weights_there)
+        gather_x(None, weights_there, None, corner)
 
     @pl.when(decodes)
     def _():
+        corner.start()
         gather_g(None, weights_there, lambda: None)
         gather_x([link.wait_recv for link in x_links], lambda: None, x_next)
         gating()
@@ -473,7 +493,7 @@
     store.start()
     end_reduce()
     store.wait()
-    for link in links + x_links + g_links + x_next + g_next:
+    for link in links + x_links + g_links + x_next + g_next + [corner]:
         link.wait_send()
 
 
@@ -638,6 +658,7 @@
         in_specs=[pl.BlockSpec(memory_space=pl.ANY)] * 4,
         out_specs=(pl.BlockSpec(memory_space=pl.ANY), whole, whole),
         scratch_shapes=[
+            vmem((2, 2) + tile, bf16),
             vmem((2, 2) + tile, bf16),
             vmem((9, 3, 128, 256), bf16),
             vmem((9, 3, 256, 128), bf16),
@@ -663,7 +684,7 @@
             vmem((1152, 512), bf16),
             vmem((3456, 256), f32),
             vmem((6912, 128), f32),
-            dma((6,)), dma((6,)), dma((6,)), dma((6,)), dma((6,)), dma((6,)), dma((6,)), dma((6,)), dma((10,)), dma((10,)),
+            dma((6,)), dma((6,)), dma((6,)), dma((6,)), dma((6,)), dma((6,)), dma((6,)), dma((6,)), dma((11,)), dma((11,)),
             vmem((ZS, YS, XS, CORES, CHUNK, 128), bf16),
             vmem((ZS, YS, XS, CHUNK, 128), bf16),
             vmem((PIECES, XS, EACH, YS, TOP, 128), bf16),

time: 84.1 us -> 81 us (0.963)
  Pallas kernels: 82.2 us -> 79.5 us
    pallas_call x1, Pallas kernels: 80.5 us -> 77.9 us  [front(): pl.pallas_call(partial(front_kernel, tms, rows_count), out_shape=(jax.Sha...]
where the time goes in v7:
time: 81 us; the launch traced here: 80.1 us
  Pallas kernels  79.5 us (98%)
    pallas_call x1, Pallas kernels, front(): pl.pallas_call(partial(front_kernel, tms, rows_count), out_shape=(jax.Sha...  77.9 us
    pallas_call x1, Pallas kernels, hand_over(): pl.pallas_call(hand_over_kernel, out_shape=(jax.ShapeDtypeStruct(sections...  1.62 us

profile of v7, /device:TPU:2, one launch (start us, length us, event | category | flops | bytes accessed | tf_op | source)
XLA Modules:
  0.0 80.1 jit_solution(5262833256771454739)
XLA Ops:
  0.6 77.9 %shard_map.67 = (bf16[2,2,128,128]{3,2,1,0:T(8,128)(2,1)}, f32[27,256]{1,0:T(8,128)}, f32[54,128]{1,0:T(8,128)}) custom-call(bf16[2,2,128,128]{3,2,1,0:T(8,128)(2,1)} %x_hbm.1, bf16[2,2,128,128]{3,2,1,0:T(8,128)(2,1)} %g_hbm.1, bf16[9,3,128,256]{3,2,1,0:T(8,128)(2,1)} %bitcast.3, bf16[9,3,256,128]{3,2,1,0:T(8,128)(2,1)} %bitcast.4), custom_call_target="tpu_custom_call" | custom-call | tf_op jit(solution)/shard_map/pallas_call | solution.py:651
  78.5 1.6 %shard_map.68 = (bf16[2,2,128,128]{3,2,1,0:T(8,128)(2,1)}, f32[1,6912]{1,0:T(1,128)}, f32[1,6912]{1,0:T(1,128)}) custom-call(bf16[2,2,128,128]{3,2,1,0:T(8,128)(2,1)} %get-tuple-element.9.sect_ref, f32[27,256]{1,0:T(8,128)} %get-tuple-element.10.in_ref, f32[54,128]{1,0:T(8,128)} %get-tuple-element.11.out_ref), custom_call_target="tpu_custom_call" | custom-call | tf_op jit(solution)/shard_map/pallas_call | solution.py:721

commit v8 on v7

--- a/solution.py
+++ b/solution.py
@@ -129,7 +129,7 @@
         load_g.start()
 
     barrier = pltpu.get_barrier_semaphore()
-    partners = [across, other, other_next, other_across, other_across_next, other_across_past, sibling, across_y] + across_x + in_time
+    partners = in_time + across_x + [across_y, other_across_next, other_across_past, other_across, other_next, other, across, sibling]
     for partner in partners:
         pl.semaphore_signal(barrier, inc=1, device_id=partner, device_id_type=MESH_ID)
     window[...] = jnp.zeros_like(window)
@@ -293,6 +293,7 @@
             products(0, i)
             products(1, i)
             far_links.append(send_edge(k, far, 0, sends))
+        for k, i in ((0, first), (1, 2 - first)):
             products(2, i)
             own_links.append(send_edge(k, own, 2, True))
         for t in range(3):
@@ -536,10 +537,10 @@
         return carry
 
     def first_copies(h):
-        copies = [
+        copies = [made(half_c.at[h, 1], got_c.at[h], s_c.at[h], r_c.at[h], across_y)]
+        return copies + [
             made(half_a.at[h, o], got_a.at[h, o], s_a.at[h, o], r_a.at[h, o], x_device(o)) for o in (2, 1, 3)
         ]
-        return copies + [made(half_c.at[h, 1], got_c.at[h], s_c.at[h], r_c.at[h], across_y)]
 
     def second_copies(h):
         copies = [made(next_a.at[h], got_a2.at[h], s_a2.at[h], r_a2.at[h], across_y)]

time: 81 us -> 80.4 us (level)
  no operation moved by 1% of the time
where the time goes in v8:
time: 80.4 us; the launch traced here: 79.8 us
  Pallas kernels  79.1 us (98%)
    pallas_call x1, Pallas kernels, front(): pl.pallas_call(partial(front_kernel, tms, rows_count), out_shape=(jax.Sha...  77.5 us
    pallas_call x1, Pallas kernels, hand_over(): pl.pallas_call(hand_over_kernel, out_shape=(jax.ShapeDtypeStruct(sections...  1.62 us

profile of v8, /device:TPU:2, one launch (start us, length us, event | category | flops | bytes accessed | tf_op | source)
XLA Modules:
  0.0 79.8 jit_solution(9321305038020485365)
XLA Ops:
  0.6 77.5 %shard_map.67 = (bf16[2,2,128,128]{3,2,1,0:T(8,128)(2,1)}, f32[27,256]{1,0:T(8,128)}, f32[54,128]{1,0:T(8,128)}) custom-call(bf16[2,2,128,128]{3,2,1,0:T(8,128)(2,1)} %x_hbm.1, bf16[2,2,128,128]{3,2,1,0:T(8,128)(2,1)} %g_hbm.1, bf16[9,3,128,256]{3,2,1,0:T(8,128)(2,1)} %bitcast.3, bf16[9,3,256,128]{3,2,1,0:T(8,128)(2,1)} %bitcast.4), custom_call_target="tpu_custom_call" | custom-call | tf_op jit(solution)/shard_map/pallas_call | solution.py:652
  78.1 1.6 %shard_map.68 = (bf16[2,2,128,128]{3,2,1,0:T(8,128)(2,1)}, f32[1,6912]{1,0:T(1,128)}, f32[1,6912]{1,0:T(1,128)}) custom-call(bf16[2,2,128,128]{3,2,1,0:T(8,128)(2,1)} %get-tuple-element.9.sect_ref, f32[27,256]{1,0:T(8,128)} %get-tuple-element.10.in_ref, f32[54,128]{1,0:T(8,128)} %get-tuple-element.11.out_ref), custom_call_target="tpu_custom_call" | custom-call | tf_op jit(solution)/shard_map/pallas_call | solution.py:722
